TPU v7x, 128 devices: a whole 4x4x4 slice. The times are simulated.
128 devices in a mesh: loc: 16 (over y, x), stream: 8 (over z, core).
Axes of the slice: x: 4, y: 4, z: 4, core: 2. Of those that a mesh axis runs over, the one named last changes fastest.
Arguments:
- latent: bfloat16 [49152, 1024], P(('loc', 'stream')), may hold values from -7 to 7
- observations: bfloat16 [8, 16, 16, 32, 1024], P('stream', 'loc'), may hold values from -7 to 7
- counts: int32 [8, 16, 16], P('stream', 'loc'), may hold values from 1 to 32, as said below
- cross_query: bfloat16 [1024, 1024], replicated, may hold values from -1 to 1
- cross_kv: bfloat16 [1024, 2048], replicated, may hold values from -1 to 1
- cross_out: bfloat16 [1024, 1024], replicated, may hold values from -0.1875 to 0.1875
- self_qkv: bfloat16 [1024, 3072], replicated, may hold values from -1 to 1
- self_out: bfloat16 [1024, 1024], replicated, may hold values from -0.1875 to 0.1875
- mlp_in: bfloat16 [1024, 4096], P(None, ('loc', 'stream')), may hold values from -0.1875 to 0.1875
- mlp_out: bfloat16 [1024, 4096], P(None, ('loc', 'stream')), may hold values from -0.09375 to 0.09375
Outputs:
- forecast: bfloat16 [49152, 1024], P(('loc', 'stream'))
Inputs may be any that keep to these rules, and one draw needn't show every extreme that they name: `counts`: slots 0 to count - 1 of a block hold observations and the rest are padding; for every stream some section receives 32 rows from every ingest shard.
All inputs are finite; a program needn't handle non-finite values.
Results may differ from a plain program's by a relative error of at most 0.013.
Values may be sent and summed in bfloat16 or wider, within the bound.
A program may use at most 192 MiB of HBM per device.

v0:
```python
import math

import jax
import jax.numpy as jnp
from jax import lax
from jax.sharding import Mesh
from jax.sharding import PartitionSpec as P

HEADS = 16
WIN = 512
STREAM = ("stream_0", "stream_1")
LOC_STREAM = ("loc", "stream_0", "stream_1")


EPSILON = 1e-06
MASKED = -1e30
BLOCK_ROWS = 512


def cut_along(shard, dim, size):
    lengths = shard.shape
    tiles = shard.reshape(*lengths[:dim], size, lengths[dim] // size, *lengths[dim + 1 :])
    return jnp.moveaxis(tiles, dim, 0)


def in_order(tiles, dim):
    lengths = list(tiles.shape[1:])
    lengths[dim] *= tiles.shape[0]
    return jnp.moveaxis(tiles, 0, dim).reshape(lengths)


def exchange_in_order(tiles, axes, order):
    lengths = [lax.axis_size(a) for a in axes]
    tiles = tiles.reshape(*lengths, *tiles.shape[1:])
    for k in order:
        tiles = lax.all_to_all(tiles, axes[k], split_axis=k, concat_axis=k, tiled=True)
    return tiles.reshape(-1, *tiles.shape[len(axes) :])


def two_step_exchange(shard, groups, order, split_dim, concat_dim):
    size = lax.axis_size(groups[0]) * lax.axis_size(groups[1])
    tiles = cut_along(shard, split_dim, size)
    return in_order(exchange_in_order(tiles, groups, order), concat_dim)


def with_halo(block, sides, width):
    for axis, dim in sides:
        count = lax.axis_size(axis)
        forward = [(i, i + 1) for i in range(count - 1)]
        backward = [(target, source) for source, target in forward]
        low = lax.ppermute(
            lax.slice_in_dim(block, block.shape[dim] - width, None, axis=dim), axis, forward
        )
        high = lax.ppermute(lax.slice_in_dim(block, 0, width, axis=dim), axis, backward)
        block = jnp.concatenate([low, block, high], axis=dim)
    return block


def rms_norm(tensor):
    floats = tensor.astype(jnp.float32)
    return (floats * lax.rsqrt(jnp.mean(floats * floats, axis=-1, keepdims=True) + EPSILON)).astype(
        jnp.bfloat16
    )


def head_split(tensor, head_count):
    return tensor.reshape(tensor.shape[0], head_count, tensor.shape[1] // head_count)


def block_size(total_rows):
    return math.gcd(total_rows, BLOCK_ROWS)


def shards(
    latent,
    observations,
    counts,
    cross_query,
    cross_kv,
    cross_out,
    self_qkv,
    self_out,
    mlp_in,
    mlp_out,
):
    node_count = latent.shape[0]
    feat_width = latent.shape[1]
    head_width = feat_width // HEADS
    score_scale = 1.0 / math.sqrt(head_width)
    slot_count = observations.shape[3]
    moved_rows, moved_counts = (
        lax.all_to_all(observations, "loc", split_axis=2, concat_axis=1, tiled=True),
        lax.all_to_all(counts.astype(jnp.bfloat16), "loc", split_axis=2, concat_axis=1, tiled=True),
    )
    block_count = moved_counts.shape[1]
    slot_index = lax.broadcasted_iota(jnp.float32, (block_count, slot_count), 1)
    live_rows = (slot_index < moved_counts.reshape(-1, 1).astype(jnp.float32)).reshape(-1)
    live_flags = live_rows.astype(jnp.bfloat16)
    kv_rows = jnp.dot(
        rms_norm(moved_rows.reshape(-1, feat_width)), cross_kv, preferred_element_type=jnp.float32
    ).astype(jnp.bfloat16)
    queries = jnp.dot(rms_norm(latent), cross_query, preferred_element_type=jnp.float32).astype(
        jnp.bfloat16
    )
    groups = lax.axis_size(STREAM)
    group_width = feat_width // groups
    group_heads = HEADS // groups
    kv_split = kv_rows.reshape(kv_rows.shape[0], 2, groups, group_width)
    live_split = jnp.broadcast_to(live_flags.reshape(-1, 1, 1), (kv_rows.shape[0], 1, groups))
    query_split = queries.reshape(node_count, 1, groups, group_width)
    kv_here, live_here, query_here = (
        lax.all_to_all(kv_split, STREAM, split_axis=2, concat_axis=0, tiled=True),
        lax.all_to_all(live_split, STREAM, split_axis=2, concat_axis=0, tiled=True),
        lax.all_to_all(query_split, STREAM, split_axis=2, concat_axis=0, tiled=True),
    )
    key_per_head = kv_here[:, 0, 0, :].reshape(-1, group_heads, head_width)
    value_per_head = kv_here[:, 1, 0, :].reshape(-1, group_heads, head_width)
    allowed = live_here.reshape(1, 1, -1) > 0
    section_rows = query_here.shape[0]
    step_rows = block_size(section_rows)
    query_blocks = query_here.reshape(section_rows // step_rows, step_rows, group_heads, head_width)

    def attend(query_block):
        score_matrix = (
            jnp.einsum(
                "jsv,esv->sje", query_block, key_per_head, preferred_element_type=jnp.float32
            )
            * score_scale
        )
        block_max = jnp.max(jnp.where(allowed, score_matrix, MASKED), axis=2, keepdims=True)
        exp_terms = jnp.where(allowed, jnp.exp(score_matrix - block_max), 0.0)
        block_sum = jnp.sum(exp_terms, axis=2)
        mixed_output = jnp.einsum(
            "lsu,uly->sly",
            exp_terms.astype(jnp.bfloat16),
            value_per_head,
            preferred_element_type=jnp.float32,
        )
        return (
            (mixed_output / jnp.transpose(block_sum)[:, :, None])
            .reshape(step_rows, 1, group_width)
            .astype(jnp.bfloat16)
        )

    head_ctx = lax.map(attend, query_blocks).reshape(section_rows, 1, group_width)
    cross_ctx = two_step_exchange(head_ctx, ("stream_0", "stream_1"), (1, 0), 0, 1).reshape(
        node_count, feat_width
    )
    after_cross = (
        latent.astype(jnp.float32)
        + jnp.dot(cross_ctx, cross_out, preferred_element_type=jnp.float32)
    ).astype(jnp.bfloat16)
    self_proj = jnp.dot(rms_norm(after_cross), self_qkv, preferred_element_type=jnp.float32).astype(
        jnp.bfloat16
    )
    half_win = WIN // 2
    window_kv = with_halo(self_proj[:, feat_width:], ((LOC_STREAM, 0),), half_win)
    first_node = lax.axis_index(LOC_STREAM) * node_count
    node_total = node_count * lax.axis_size(LOC_STREAM)
    query_pos = first_node + lax.broadcasted_iota(jnp.int32, (node_count, 1), 0)
    key_pos = (
        first_node - half_win + lax.broadcasted_iota(jnp.int32, (1, node_count + 2 * half_win), 1)
    )
    window_mask = (
        (jnp.abs(query_pos - key_pos) <= half_win) & (key_pos >= 0) & (key_pos < node_total)
    )
    score_matrix = (
        jnp.einsum(
            "jsv,esv->sje",
            head_split(self_proj[:, :feat_width], HEADS),
            head_split(window_kv[:, :feat_width], HEADS),
            preferred_element_type=jnp.float32,
        )
        * score_scale
    )
    score_matrix = jnp.where(window_mask[None], score_matrix, MASKED)
    window_max = jnp.max(score_matrix, axis=2, keepdims=True)
    exp_terms = jnp.where(window_mask[None], jnp.exp(score_matrix - window_max), 0.0)
    window_sum = jnp.sum(exp_terms, axis=2)
    mixed_output = jnp.einsum(
        "lsu,uly->sly",
        exp_terms.astype(jnp.bfloat16),
        head_split(window_kv[:, feat_width:], HEADS),
        preferred_element_type=jnp.float32,
    )
    self_ctx = (
        (mixed_output / jnp.transpose(window_sum)[:, :, None])
        .reshape(node_count, feat_width)
        .astype(jnp.bfloat16)
    )
    after_self = (
        after_cross.astype(jnp.float32)
        + jnp.dot(self_ctx, self_out, preferred_element_type=jnp.float32)
    ).astype(jnp.bfloat16)
    mlp_norm = rms_norm(after_self)
    weight_in = lax.all_gather(mlp_in, LOC_STREAM, axis=1, tiled=True)
    weight_back = lax.all_gather(mlp_out, LOC_STREAM, axis=1, tiled=True)
    hidden = jax.nn.gelu(
        jnp.dot(mlp_norm, weight_in, preferred_element_type=jnp.float32), approximate=True
    ).astype(jnp.bfloat16)
    mlp_sum = lax.dot_general(
        hidden, weight_back, (((1,), (1,)), ((), ())), preferred_element_type=jnp.float32
    )
    return (after_self.astype(jnp.float32) + mlp_sum).astype(jnp.bfloat16)


def solution(mesh):
    finer = Mesh(mesh.devices.reshape(mesh.shape["loc"], 4, 2), ("loc", "stream_0", "stream_1"))
    return jax.shard_map(
        shards,
        mesh=finer,
        in_specs=(
            P(LOC_STREAM, None),
            P(STREAM, "loc", None, None, None),
            P(STREAM, "loc", None),
            P(),
            P(),
            P(),
            P(),
            P(),
            P(None, LOC_STREAM),
            P(None, LOC_STREAM),
        ),
        out_specs=P(LOC_STREAM, None),
        check_vma=False,
    )
```

profile of v0, /device:TPU:8, one launch (start us, length us, event | category | flops | bytes accessed | tf_op | source)
XLA Modules:
  0.0 329.6 jit_solution(445264827035118089)
XLA Ops:
  8.6 7.4 %all-to-all-start = ((bf16[1,1,16]{1,0,2:T(2,128)(2,1)}), bf16[1,1,16]{1,0,2:T(2,128)(2,1)S(1)}, u32[]{:S(2)}, u32[]{:S(2)}) async-start(bf16[1,1,16]{1,0,2:T(2,128)(2,1)} %copy.50), calls=%async_computation | async-start | bytes 16384 | tf_op jit(solution)/shard_map/all_to_all | solution.py:93
  35.3 5.5 %all-to-all-done.3 = bf16[1,1,16,32,1024]{4,3,1,0,2:T(8,128)(2,1)S(1)} async-done(((bf16[1,1,16,32,1024]{4,3,1,0,2:T(8,128)(2,1)}), bf16[1,1,16,32,1024]{4,3,1,0,2:T(8,128)(2,1)S(1)}, u32[]{:S(2)}, u32[]{:S(2)}) %all-to-all-start.3) | async-done | bytes 1048608 | tf_op jit(solution)/shard_map/all_to_all | solution.py:92
  63.0 6.6 %all-to-all-done.2 = bf16[384,1,8,128]{0,3,1,2:T(8,128)(2,1)} async-done(((bf16[384,1,8,128]{0,3,1,2:T(8,128)(2,1)}), bf16[384,1,8,128]{0,3,1,2:T(8,128)(2,1)}, u32[]{:S(2)}, u32[]{:S(2)}) %all-to-all-start.2) | async-done | bytes 786464 | tf_op jit(solution)/shard_map/all_to_all | solution.py:114
  80.1 29.2 %all-to-all-done.4 = bf16[512,2,8,128]{3,0,1,2:T(8,128)(2,1)} async-done(((bf16[512,2,8,128]{3,0,1,2:T(8,128)(2,1)}), bf16[512,2,8,128]{3,0,1,2:T(8,128)(2,1)}, u32[]{:S(2)}, u32[]{:S(2)}) %all-to-all-start.4) | async-done | bytes 2097184 | tf_op jit(solution)/shard_map/all_to_all | solution.py:112
  115.0 102.9 %while.10 = (s32[]{:T(128)}, bf16[6,512,1,128]{3,1,0,2:T(8,128)(2,1)}, pred[1,1,4096]{2,1,0:T(4,128)(4,1)S(1)}, bf16[6,512,2,64]{1,3,2,0:T(8,128)(2,1)}, bf16[40...) while((s32[]{:T(128)}, bf16[6,512,1,128]{3,1,0,2:T(8,128)(2,1)}, ...), condition=%wide.region_5.6_spmd, body=%wide.region_2.5_spmd.sunk | while | flops 1640108032 | bytes 20866644 | solution.py:145
  115.0 10.2 %fusion.143 = (f32[2,512]{1,0:T(2,128)S(1)}, bf16[2,512,4096]{2,1,0:T(8,128)(2,1)}) fusion(pred[4096]{0:T(1024)(128)(4,1)S(1)} %reduce.8, bf16[4096,2,64]{0,2,1:T(8,128)(2,1)} %get-tuple-element.155, bf16[6,512,2,64]{1,3,2,0:T(8,128)(2,1)} %get-tuple-element.154, s32[]{:T(128)} %get-tuple-element.143), kind=kOutput, calls=%fused_computation.101.clone.1 | convolution fusion | flops 1103106048 | bytes 10761216 | tf_op jit(solution)/shard_map/while/body/eval_jaxpr/sub | solution.py:131
  125.2 6.0 %fusion.144 = bf16[512,2,64]{0,2,1:T(8,128)(2,1)S(1)} fusion(bf16[4096,2,64]{0,2,1:T(8,128)(2,1)S(1)} %get-tuple-element.156, bf16[2,512,4096]{2,1,0:T(8,128)(2,1)} %get-tuple-element.133, f32[512,2]{0,1:T(2,128)S(1)} %bitcast.122), kind=kOutput, calls=%fused_computation.13.clone.1 | convolution fusion | flops 537001984 | bytes 9572352 | tf_op jit(solution)/shard_map/while/body/eval_jaxpr/lsu,uly->sly/dot_general | solution.py:133
  132.1 10.2 %fusion.143 = (f32[2,512]{1,0:T(2,128)S(1)}, bf16[2,512,4096]{2,1,0:T(8,128)(2,1)}) fusion(pred[4096]{0:T(1024)(128)(4,1)S(1)} %reduce.8, bf16[4096,2,64]{0,2,1:T(8,128)(2,1)} %get-tuple-element.155, bf16[6,512,2,64]{1,3,2,0:T(8,128)(2,1)} %get-tuple-element.154, s32[]{:T(128)} %get-tuple-element.143), kind=kOutput, calls=%fused_computation.101.clone.1 | convolution fusion | flops 1103106048 | bytes 10761216 | tf_op jit(solution)/shard_map/while/body/eval_jaxpr/sub | solution.py:131
  142.3 6.1 %fusion.144 = bf16[512,2,64]{0,2,1:T(8,128)(2,1)S(1)} fusion(bf16[4096,2,64]{0,2,1:T(8,128)(2,1)S(1)} %get-tuple-element.156, bf16[2,512,4096]{2,1,0:T(8,128)(2,1)} %get-tuple-element.133, f32[512,2]{0,1:T(2,128)S(1)} %bitcast.122), kind=kOutput, calls=%fused_computation.13.clone.1 | convolution fusion | flops 537001984 | bytes 9572352 | tf_op jit(solution)/shard_map/while/body/eval_jaxpr/lsu,uly->sly/dot_general | solution.py:133
  149.2 10.2 %fusion.143 = (f32[2,512]{1,0:T(2,128)S(1)}, bf16[2,512,4096]{2,1,0:T(8,128)(2,1)}) fusion(pred[4096]{0:T(1024)(128)(4,1)S(1)} %reduce.8, bf16[4096,2,64]{0,2,1:T(8,128)(2,1)} %get-tuple-element.155, bf16[6,512,2,64]{1,3,2,0:T(8,128)(2,1)} %get-tuple-element.154, s32[]{:T(128)} %get-tuple-element.143), kind=kOutput, calls=%fused_computation.101.clone.1 | convolution fusion | flops 1103106048 | bytes 10761216 | tf_op jit(solution)/shard_map/while/body/eval_jaxpr/sub | solution.py:131
  159.4 6.6 %fusion.144 = bf16[512,2,64]{0,2,1:T(8,128)(2,1)S(1)} fusion(bf16[4096,2,64]{0,2,1:T(8,128)(2,1)S(1)} %get-tuple-element.156, bf16[2,512,4096]{2,1,0:T(8,128)(2,1)} %get-tuple-element.133, f32[512,2]{0,1:T(2,128)S(1)} %bitcast.122), kind=kOutput, calls=%fused_computation.13.clone.1 | convolution fusion | flops 537001984 | bytes 9572352 | tf_op jit(solution)/shard_map/while/body/eval_jaxpr/lsu,uly->sly/dot_general | solution.py:133
  166.8 10.1 %fusion.143 = (f32[2,512]{1,0:T(2,128)S(1)}, bf16[2,512,4096]{2,1,0:T(8,128)(2,1)}) fusion(pred[4096]{0:T(1024)(128)(4,1)S(1)} %reduce.8, bf16[4096,2,64]{0,2,1:T(8,128)(2,1)} %get-tuple-element.155, bf16[6,512,2,64]{1,3,2,0:T(8,128)(2,1)} %get-tuple-element.154, s32[]{:T(128)} %get-tuple-element.143), kind=kOutput, calls=%fused_computation.101.clone.1 | convolution fusion | flops 1103106048 | bytes 10761216 | tf_op jit(solution)/shard_map/while/body/eval_jaxpr/sub | solution.py:131
  177.0 6.0 %fusion.144 = bf16[512,2,64]{0,2,1:T(8,128)(2,1)S(1)} fusion(bf16[4096,2,64]{0,2,1:T(8,128)(2,1)S(1)} %get-tuple-element.156, bf16[2,512,4096]{2,1,0:T(8,128)(2,1)} %get-tuple-element.133, f32[512,2]{0,1:T(2,128)S(1)} %bitcast.122), kind=kOutput, calls=%fused_computation.13.clone.1 | convolution fusion | flops 537001984 | bytes 9572352 | tf_op jit(solution)/shard_map/while/body/eval_jaxpr/lsu,uly->sly/dot_general | solution.py:133
  183.9 10.1 %fusion.143 = (f32[2,512]{1,0:T(2,128)S(1)}, bf16[2,512,4096]{2,1,0:T(8,128)(2,1)}) fusion(pred[4096]{0:T(1024)(128)(4,1)S(1)} %reduce.8, bf16[4096,2,64]{0,2,1:T(8,128)(2,1)} %get-tuple-element.155, bf16[6,512,2,64]{1,3,2,0:T(8,128)(2,1)} %get-tuple-element.154, s32[]{:T(128)} %get-tuple-element.143), kind=kOutput, calls=%fused_computation.101.clone.1 | convolution fusion | flops 1103106048 | bytes 10761216 | tf_op jit(solution)/shard_map/while/body/eval_jaxpr/sub | solution.py:131
  194.0 6.0 %fusion.144 = bf16[512,2,64]{0,2,1:T(8,128)(2,1)S(1)} fusion(bf16[4096,2,64]{0,2,1:T(8,128)(2,1)S(1)} %get-tuple-element.156, bf16[2,512,4096]{2,1,0:T(8,128)(2,1)} %get-tuple-element.133, f32[512,2]{0,1:T(2,128)S(1)} %bitcast.122), kind=kOutput, calls=%fused_computation.13.clone.1 | convolution fusion | flops 537001984 | bytes 9572352 | tf_op jit(solution)/shard_map/while/body/eval_jaxpr/lsu,uly->sly/dot_general | solution.py:133
  200.9 10.1 %fusion.143 = (f32[2,512]{1,0:T(2,128)S(1)}, bf16[2,512,4096]{2,1,0:T(8,128)(2,1)}) fusion(pred[4096]{0:T(1024)(128)(4,1)S(1)} %reduce.8, bf16[4096,2,64]{0,2,1:T(8,128)(2,1)} %get-tuple-element.155, bf16[6,512,2,64]{1,3,2,0:T(8,128)(2,1)} %get-tuple-element.154, s32[]{:T(128)} %get-tuple-element.143), kind=kOutput, calls=%fused_computation.101.clone.1 | convolution fusion | flops 1103106048 | bytes 10761216 | tf_op jit(solution)/shard_map/while/body/eval_jaxpr/sub | solution.py:131
  211.1 6.0 %fusion.144 = bf16[512,2,64]{0,2,1:T(8,128)(2,1)S(1)} fusion(bf16[4096,2,64]{0,2,1:T(8,128)(2,1)S(1)} %get-tuple-element.156, bf16[2,512,4096]{2,1,0:T(8,128)(2,1)} %get-tuple-element.133, f32[512,2]{0,1:T(2,128)S(1)} %bitcast.122), kind=kOutput, calls=%fused_computation.13.clone.1 | convolution fusion | flops 537001984 | bytes 9572352 | tf_op jit(solution)/shard_map/while/body/eval_jaxpr/lsu,uly->sly/dot_general | solution.py:133
  223.5 15.3 %all_to_all.71 = bf16[4,2,384,1,128]{4,2,1,3,0:T(8,128)(2,1)S(1)} all-to-all(bf16[4,2,384,1,128]{4,2,1,3,0:T(8,128)(2,1)S(1)} %copy.62), channel_id=1, replica_groups=mesh['loc'=16,'stream_0'=4,'stream_1'=2] {'stream_0'}, dimensions={0} | all-to-all | bytes 1572864 | tf_op jit(solution)/shard_map/all_to_all | solution.py:36
  242.5 6.0 %convolution_convert_fusion = bf16[384,3072]{1,0:T(8,128)(2,1)S(1)} fusion(bf16[1024,3072]{1,0:T(8,128)(2,1)} %param.18, bf16[384,1024]{1,0:T(8,128)(2,1)S(1)} %get-tuple-element.83, f32[384]{0:T(512)S(1)} %add_rsqrt_fusion.2), kind=kOutput, calls=%fused_computation.42 | convolution fusion | flops 2418278400 | bytes 9438720 | tf_op jit(solution)/shard_map/dot_general | solution.py:153
  253.5 8.1 %collective-permute-start.1 = (bf16[256,2048]{1,0:T(8,128)(2,1)}, bf16[256,2048]{1,0:T(8,128)(2,1)}, u32[]{:S(2)}, u32[]{:S(2)}) collective-permute-start(bf16[256,2048]{1,0:T(8,128)(2,1)} %get-tuple-element.79), channel_id=1, source_target_pairs={{1,0},{2,1},{3,2},{4,3},{5,4},{6,5},{7,6},{8,7},{9,8},{10,9},{11,1... | collective-permute-start | bytes 3145736 | tf_op jit(solution)/shard_map/ppermute | solution.py:54
  266.1 6.2 %collective-permute-done = bf16[256,2048]{1,0:T(8,128)(2,1)} collective-permute-done((bf16[256,2048]{1,0:T(8,128)(2,1)}, bf16[256,2048]{1,0:T(8,128)(2,1)}, u32[]{:S(2)}, u32[]{:S(2)}) %collective-permute-start) | collective-permute-done | bytes 1048608 | tf_op jit(solution)/shard_map/ppermute | solution.py:51
  286.2 13.1 %fusion.108 = (f32[16,384]{1,0:T(8,128)S(1)}, bf16[16,384,896]{2,1,0:T(8,128)(2,1)}) fusion(pred[384,896]{1,0:T(8,128)(4,1)S(1)} %fusion.76, bf16[384,16,64]{0,2,1:T(8,128)(2,1)S(1)} %bitcast.120, bf16[896,16,64]{0,2,1:T(8,128)(2,1)} %bitcast.115), kind=kOutput, calls=%fused_computation.105 | convolution fusion | flops 737674112 | bytes 14000128 | tf_op jit(solution)/shard_map/sub | solution.py:178
  299.3 8.4 %fusion.70 = bf16[384,16,64]{0,2,1:T(8,128)(2,1)S(1)} fusion(bf16[896,16,64]{0,2,1:T(8,128)(2,1)} %bitcast.116, bf16[16,384,896]{2,1,0:T(8,128)(2,1)} %get-tuple-element.85, f32[384,16]{0,1:T(8,128)S(1)} %bitcast.124), kind=kOutput, calls=%fused_computation.73 | convolution fusion | flops 705429504 | bytes 13656064 | tf_op jit(solution)/shard_map/lsu,uly->sly/dot_general | solution.py:180
  308.9 13.8 %fusion.69 = bf16[384,1024]{1,0:T(8,128)(2,1)} fusion(bf16[384,1024]{1,0:T(8,128)(2,1)S(1)} %get-tuple-element.87, bf16[1024,4096]{0,1:T(8,128)(2,1)} %all-gather.5.cloned.1.call-done, bf16[1024,4096]{0,1:T(8,128)(2,1)} %all-gather.3.cloned.1.call-done, f32[384]{0:T(512)S(1)} %add_rsqrt_fusion.1), kind=kOutput, calls=%fused_computation.71 | convolution fusion | flops 6458966016 | bytes 18351616 | tf_op jit(solution)/shard_map/dot_general | solution.py:201
  (96 shorter events, 98.4 us)
Async XLA Ops:
  6.5 233.4 %copy-start = (bf16[1024,1024]{1,0:T(8,128)(2,1)S(1)}, bf16[1024,1024]{1,0:T(8,128)(2,1)}, u32[]{:S(2)}) copy-start(bf16[1024,1024]{1,0:T(8,128)(2,1)} %param.17) | copy-start | bytes 6291460
  6.5 302.4 %all-gather.3.cloned.1.call-start = ((), (), s32[]{:S(2)}) async-start(), calls=%async_computation.7 | async-start | bytes 8454144 | tf_op jit(solution)/shard_map/all_gather | solution.py:196
  8.6 13.5 %all-to-all-start = ((bf16[1,1,16]{1,0,2:T(2,128)(2,1)}), bf16[1,1,16]{1,0,2:T(2,128)(2,1)S(1)}, u32[]{:S(2)}, u32[]{:S(2)}) async-start(bf16[1,1,16]{1,0,2:T(2,128)(2,1)} %copy.50), calls=%async_computation | async-start | bytes 16384 | tf_op jit(solution)/shard_map/all_to_all | solution.py:93
  22.1 18.8 %all-to-all-start.3 = ((bf16[1,1,16,32,1024]{4,3,1,0,2:T(8,128)(2,1)}), bf16[1,1,16,32,1024]{4,3,1,0,2:T(8,128)(2,1)S(1)}, u32[]{:S(2)}, u32[]{:S(2)}) async-start(bf16[1,1,16,32,1024]{4,3,1,0,2:T(8,128)(2,1)} %bitcast.117), calls=%async_computation.3 | async-start | bytes 2097152 | tf_op jit(solution)/shard_map/all_to_all | solution.py:92
  40.9 10.6 %all-to-all-start.1 = ((bf16[8,2,256]{2,1,0:T(2,128)(2,1)}), bf16[8,2,256]{2,1,0:T(2,128)(2,1)S(1)}, u32[]{:S(2)}, u32[]{:S(2)}) async-start(bf16[8,2,256]{2,1,0:T(2,128)(2,1)} %reshape.235), calls=%async_computation.1 | async-start | bytes 16384 | tf_op jit(solution)/shard_map/all_to_all | solution.py:113
  51.5 18.2 %all-to-all-start.2 = ((bf16[384,1,8,128]{0,3,1,2:T(8,128)(2,1)}), bf16[384,1,8,128]{0,3,1,2:T(8,128)(2,1)}, u32[]{:S(2)}, u32[]{:S(2)}) async-start(bf16[384,1,8,128]{0,3,1,2:T(8,128)(2,1)} %bitcast.112), calls=%async_computation.2 | async-start | bytes 1572864 | tf_op jit(solution)/shard_map/all_to_all | solution.py:114
  69.6 39.6 %all-to-all-start.4 = ((bf16[512,2,8,128]{3,0,1,2:T(8,128)(2,1)}), bf16[512,2,8,128]{3,0,1,2:T(8,128)(2,1)}, u32[]{:S(2)}, u32[]{:S(2)}) async-start(bf16[512,2,8,128]{3,0,1,2:T(8,128)(2,1)} %copy.55), calls=%async_computation.4 | async-start | bytes 4194304 | tf_op jit(solution)/shard_map/all_to_all | solution.py:112
  74.1 234.8 %all-gather.5.cloned.1.call-start = ((), (), s32[]{:S(2)}) async-start(), calls=%async_computation.8 | async-start | bytes 8454144 | tf_op jit(solution)/shard_map/all_gather | solution.py:197
  242.4 6.0 %copy-start.2 = (bf16[384,1024]{1,0:T(8,128)(2,1)}, bf16[384,1024]{1,0:T(8,128)(2,1)S(1)}, u32[]{:S(2)}) copy-start(bf16[384,1024]{1,0:T(8,128)(2,1)S(1)} %get-tuple-element.83) | copy-start | bytes 2359300
  248.5 1.4 copy-start.1
  251.5 13.4 %slice-start = ((bf16[384,3072]{1,0:T(8,128)(2,1)}), bf16[384,1024]{1,0:T(8,128)(2,1)S(1)}, s32[]{:S(2)}) async-start(bf16[384,3072]{1,0:T(8,128)(2,1)} %copy-done.1), calls=%async_computation.9 | async-start | bytes 1572864 | tf_op jit(solution)/shard_map/slice | solution.py:170
  251.5 20.8 %collective-permute-start = (bf16[256,2048]{1,0:T(8,128)(2,1)}, bf16[256,2048]{1,0:T(8,128)(2,1)}, u32[]{:S(2)}, u32[]{:S(2)}) collective-permute-start(bf16[256,2048]{1,0:T(8,128)(2,1)} %get-tuple-element.78), channel_id=1, source_target_pairs={{0,1},{1,2},{2,3},{3,4},{4,5},{5,6},{6,7},{7,8},{8,9},{9,10},{10,1... | collective-permute-start | bytes 3145736 | tf_op jit(solution)/shard_map/ppermute | solution.py:51
  253.5 20.5 %collective-permute-start.1 = (bf16[256,2048]{1,0:T(8,128)(2,1)}, bf16[256,2048]{1,0:T(8,128)(2,1)}, u32[]{:S(2)}, u32[]{:S(2)}) collective-permute-start(bf16[256,2048]{1,0:T(8,128)(2,1)} %get-tuple-element.79), channel_id=1, source_target_pairs={{1,0},{2,1},{3,2},{4,3},{5,4},{6,5},{7,6},{8,7},{9,8},{10,9},{11,1... | collective-permute-start | bytes 3145736 | tf_op jit(solution)/shard_map/ppermute | solution.py:54
  278.5 7.7 %copy-start.5 = (bf16[384,1024]{0,1:T(8,128)(2,1)S(1)}, bf16[384,1024]{0,1:T(8,128)(2,1)}, u32[]{:S(2)}) copy-start(bf16[384,1024]{0,1:T(8,128)(2,1)} %copy.65) | copy-start | bytes 2359300
  299.3 8.5 %copy-start.3 = (bf16[384,1024]{1,0:T(8,128)(2,1)S(1)}, bf16[384,1024]{1,0:T(8,128)(2,1)}, u32[]{:S(2)}) copy-start(bf16[384,1024]{1,0:T(8,128)(2,1)} %copy-done.2) | copy-start | bytes 2359300
  299.3 8.5 %copy-start.4 = (bf16[1024,1024]{1,0:T(8,128)(2,1)S(1)}, bf16[1024,1024]{1,0:T(8,128)(2,1)}, u32[]{:S(2)}) copy-start(bf16[1024,1024]{1,0:T(8,128)(2,1)} %param.19) | copy-start | bytes 6291460
Sparse Core Ops, SparseCore 0:
  10.3 88.9 all-gather.2
  102.3 69.9 all-gather.4
where the time goes:
time: 332 us; the launch traced here: 330 us
  matrix products  151 us (45%)
  waiting for transfers between devices  60.3 us (18%)
  local copies, waits for them, and re-layouts  41.7 us (13%)
  starting transfers between devices  36.6 us (11%)
  blocking collectives  19.6 us (6%)
  between operations  13.7 us (4%)
  other arithmetic  6.6 us (2%)
    sub x6, matrix products, attend(): exp_terms = jnp.where(allowed, jnp.exp(score_matrix - block_max), 0.0)  61 us
    dot_general x6, matrix products, attend(): jnp.einsum('lsu,uly->sly', exp_terms.astype(jnp.bfloat16), value_per_head...  36.8 us
    all_to_all x1, waiting for transfers between devices, shards(): lax.all_to_all(kv_split, STREAM, split_axis=2, concat_axis=0, tiled=True)  29.2 us
    all_to_all x2, blocking collectives, exchange_in_order(): lax.all_to_all(tiles, axes[k], split_axis=k, concat_axis=k, tiled=True)  19.6 us
    dot_general x1, matrix products, shards(): lax.dot_general(hidden, weight_back, (((1,), (1,)), ((), ())), preferred_...  13.8 us
    sub x1, matrix products, shards(): score_matrix - window_max  13.1 us
    dot_general x1, matrix products, shards(): jnp.einsum('lsu,uly->sly', exp_terms.astype(jnp.bfloat16), head_split(win...  8.45 us
    ppermute x1, starting transfers between devices, with_halo(): lax.ppermute(lax.slice_in_dim(block, 0, width, axis=dim), axis, backward)  8.08 us
  transfers between devices with their start and end apart: 9, of which 7 were waited for; matrix products, arithmetic and copies ran while one was open for 56% of the time, Pallas kernels for 0%

commit v1 on v0

v1 whole, which is shorter than its diff:
```python
import functools
import math

import jax
import jax.numpy as jnp
from jax import lax
from jax.experimental import pallas as pl
from jax.experimental.pallas import tpu as pltpu
from jax.sharding import Mesh
from jax.sharding import PartitionSpec as P

HEADS = 16
HEAD = 64
PAIR = 128
GROUPS = 8
WIN = 512
LOC = 16
CAP = 32
STREAM = ("s0", "s1")
LOC_STREAM = ("loc", "s0", "s1")
EPSILON = 1e-06
MASKED = -1e30
PADDING = 1e30
PADDING_FROM = 1e29
QSCALE = math.log2(math.e) / math.sqrt(HEAD)
MESH = pl.DeviceIdType.MESH
F32 = jnp.float32
BF16 = jnp.bfloat16
NT = (((1,), (1,)), ((), ()))
VMEM_LIMIT = 56 << 20


def params(**more):
    return pltpu.CompilerParams(vmem_limit_bytes=VMEM_LIMIT, **more)


def rms_norm(tensor):
    floats = tensor.astype(F32)
    return (floats * lax.rsqrt(jnp.mean(floats * floats, axis=-1, keepdims=True) + EPSILON)).astype(
        BF16
    )


def project_kernel(counts, obs, latent, wk, wv, wq, kv_out, q_out, xn, ln):
    @pl.when(pl.program_id(0) == 0)
    def _():
        xn[...] = rms_norm(obs[...])
        ln[...] = rms_norm(latent[...])

    q = (jnp.dot(ln[...], wq[...], preferred_element_type=F32) * QSCALE).astype(BF16)
    k = jnp.dot(xn[...], wk[...], preferred_element_type=F32)
    v = jnp.dot(xn[...], wv[...], preferred_element_type=F32)
    slot = lax.broadcasted_iota(jnp.int32, (CAP, PAIR), 0)
    for s in range(LOC):
        live = slot < counts[s]
        rows = slice(s * CAP, (s + 1) * CAP)
        for g in range(2):
            columns = slice(g * PAIR, (g + 1) * PAIR)
            kv_out[s, g, :, 0:PAIR] = jnp.where(live, k[rows, columns], PADDING).astype(BF16)
            kv_out[s, g, :, PAIR:] = jnp.where(live, v[rows, columns], PADDING).astype(BF16)
    for g in range(2):
        q_out[g] = q[:, g * PAIR : (g + 1) * PAIR]


def project(counts, obs, latent, cross_kv, cross_query):
    rows, width = obs.shape
    nodes = latent.shape[0]
    step = 2 * PAIR
    steps = width // step
    return pl.pallas_call(
        project_kernel,
        grid=(steps,),
        out_shape=(
            jax.ShapeDtypeStruct((LOC, GROUPS, CAP, 2 * PAIR), BF16),
            jax.ShapeDtypeStruct((GROUPS, nodes, PAIR), BF16),
        ),
        in_specs=[
            pl.BlockSpec(memory_space=pltpu.SMEM),
            pl.BlockSpec((rows, width), lambda j: (0, 0)),
            pl.BlockSpec((nodes, width), lambda j: (0, 0)),
            pl.BlockSpec((width, step), lambda j: (0, j)),
            pl.BlockSpec((width, step), lambda j: (0, j + steps)),
            pl.BlockSpec((width, step), lambda j: (0, j)),
        ],
        out_specs=(
            pl.BlockSpec((LOC, 2, CAP, 2 * PAIR), lambda j: (0, j, 0, 0)),
            pl.BlockSpec((2, nodes, PAIR), lambda j: (j, 0, 0)),
        ),
        scratch_shapes=[pltpu.VMEM((rows, width), BF16), pltpu.VMEM((nodes, width), BF16)],
        compiler_params=params(),
        name="project",
    )(counts, obs, latent, cross_kv, cross_kv, cross_query)


def exchange_kernel(kv, q, kv_here, q_here, kv_send, kv_recv, q_send, q_recv):
    loc = lax.axis_index("loc")
    me = lax.axis_index("s0") * 2 + lax.axis_index("s1")
    mine = loc * GROUPS + me
    pltpu.make_async_copy(q.at[me], q_here.at[me], q_recv).start()
    pltpu.make_async_copy(kv.at[mine], kv_here.at[me * LOC + loc], kv_recv).start()

    @pl.loop(1, GROUPS)
    def _(d):
        to = lax.rem(me + d, GROUPS)
        pltpu.make_async_remote_copy(
            q.at[to],
            q_here.at[me],
            q_send,
            q_recv,
            device_id=(loc, to // 2, lax.rem(to, 2)),
            device_id_type=MESH,
        ).start()

    @pl.loop(1, LOC * GROUPS)
    def _(d):
        to = lax.rem(mine + d, LOC * GROUPS)
        section = to // GROUPS
        group = lax.rem(to, GROUPS)
        pltpu.make_async_remote_copy(
            kv.at[to],
            kv_here.at[me * LOC + loc],
            kv_send,
            kv_recv,
            device_id=(section, group // 2, lax.rem(group, 2)),
            device_id_type=MESH,
        ).start()

    pltpu.make_async_copy(q.at[pl.ds(0, GROUPS - 1)], q_here.at[pl.ds(0, GROUPS - 1)], q_send).wait()
    pltpu.make_async_copy(q, q_here, q_recv).wait()

    sent = pl.ds(0, LOC * GROUPS - 1)
    pltpu.make_async_copy(kv.at[sent], kv_here.at[sent], kv_send).wait()
    pltpu.make_async_copy(kv_here, kv_here, kv_recv).wait()


def exchange(kv, q):
    return pl.pallas_call(
        exchange_kernel,
        out_shape=(
            jax.ShapeDtypeStruct(kv.shape, BF16),
            jax.ShapeDtypeStruct(q.shape, BF16),
        ),
        in_specs=[pl.BlockSpec(memory_space=pl.ANY)] * 2,
        out_specs=(pl.BlockSpec(memory_space=pl.ANY),) * 2,
        scratch_shapes=[pltpu.SemaphoreType.DMA] * 4,
        compiler_params=params(has_side_effects=True),
        name="exchange",
    )(kv, q)


def give_back_kernel(ctx, ctx_here, send, recv):
    loc = lax.axis_index("loc")
    me = lax.axis_index("s0") * 2 + lax.axis_index("s1")
    pltpu.make_async_copy(ctx.at[me], ctx_here.at[me], recv).start()

    @pl.loop(1, GROUPS)
    def _(d):
        to = lax.rem(me + d, GROUPS)
        pltpu.make_async_remote_copy(
            ctx.at[to],
            ctx_here.at[me],
            send,
            recv,
            device_id=(loc, to // 2, lax.rem(to, 2)),
            device_id_type=MESH,
        ).start()

    pltpu.make_async_copy(ctx.at[pl.ds(0, GROUPS - 1)], ctx_here.at[pl.ds(0, GROUPS - 1)], send).wait()
    pltpu.make_async_copy(ctx, ctx_here, recv).wait()


def give_back(ctx):
    return pl.pallas_call(
        give_back_kernel,
        out_shape=jax.ShapeDtypeStruct(ctx.shape, BF16),
        in_specs=[pl.BlockSpec(memory_space=pl.ANY)],
        out_specs=pl.BlockSpec(memory_space=pl.ANY),
        scratch_shapes=[pltpu.SemaphoreType.DMA] * 2,
        compiler_params=params(has_side_effects=True),
        name="give_back",
    )(ctx)


def lane_max(scores, width):
    top = scores[:, 0:PAIR]
    for c in range(1, width // PAIR):
        top = jnp.maximum(top, scores[:, c * PAIR : (c + 1) * PAIR])
    return top


def cross_kernel(tile, kv, q, out, k0, k1, v0, v1, s0, s1):
    rows = kv.shape[0]
    block = q.shape[0]

    @pl.when(pl.program_id(0) == 0)
    def _():
        prep = 512
        lane = lax.broadcasted_iota(jnp.int32, (prep, PAIR), 1)
        low = lane < HEAD

        @pl.loop(0, rows // prep)
        def _(b):
            at = pl.ds(pl.multiple_of(b * prep, prep), prep)
            key = kv[at, 0:PAIR].astype(F32)
            value = kv[at, PAIR:].astype(F32)
            live = key < PADDING_FROM
            bias = jnp.where(live, 0.0, MASKED)
            key = jnp.where(live, key, 0.0)
            value = jnp.where(live, value, 0.0)
            first = jnp.where(low, key, jnp.where(lane == HEAD, bias, 0.0))
            second = jnp.where(low, jnp.where(lane == 0, bias, 0.0), key)
            k0[:, at] = jnp.transpose(first).astype(BF16)
            k1[:, at] = jnp.transpose(second).astype(BF16)
            v0[at, :] = jnp.where(low, value, 1.0).astype(BF16)
            v1[at, :] = jnp.where(low, 1.0, value).astype(BF16)

    lane = lax.broadcasted_iota(jnp.int32, (block, PAIR), 1)
    low = lane < HEAD
    both = q[...].astype(F32)
    q0 = jnp.where(low, both, jnp.where(lane == HEAD, 1.0, 0.0)).astype(BF16)
    q1 = jnp.where(low, jnp.where(lane == 0, 1.0, 0.0), both).astype(BF16)
    lowest = jnp.full((block, PAIR), -3e38, F32)

    def score(b, tops):
        at = pl.ds(pl.multiple_of(b * tile, tile), tile)
        a0 = jnp.dot(q0, k0[:, at], preferred_element_type=F32)
        s0[:, at] = a0
        a1 = jnp.dot(q1, k1[:, at], preferred_element_type=F32)
        s1[:, at] = a1
        return (
            jnp.maximum(tops[0], lane_max(a0, tile)),
            jnp.maximum(tops[1], lane_max(a1, tile)),
        )

    tops = lax.fori_loop(0, rows // tile, score, (lowest, lowest))
    m0 = jnp.max(tops[0], axis=1, keepdims=True)
    m1 = jnp.max(tops[1], axis=1, keepdims=True)

    def mix(b, totals):
        at = pl.ds(pl.multiple_of(b * tile, tile), tile)
        p0 = jnp.exp2(s0[:, at] - m0).astype(BF16)
        p1 = jnp.exp2(s1[:, at] - m1).astype(BF16)
        return (
            totals[0] + jnp.dot(p0, v0[at, :], preferred_element_type=F32),
            totals[1] + jnp.dot(p1, v1[at, :], preferred_element_type=F32),
        )

    zero = jnp.zeros((block, PAIR), F32)
    t0, t1 = lax.fori_loop(0, rows // tile, mix, (zero, zero))
    sums = pltpu.roll(jnp.where(low, t1, t0), HEAD, 1)
    out[...] = (jnp.where(low, t0, t1) / sums).astype(BF16)


def cross_attention(kv, q, block=256, tile=512):
    rows = kv.shape[0]
    nodes = q.shape[0]
    return pl.pallas_call(
        functools.partial(cross_kernel, tile),
        grid=(nodes // block,),
        out_shape=jax.ShapeDtypeStruct(q.shape, BF16),
        in_specs=[
            pl.BlockSpec((rows, 2 * PAIR), lambda j: (0, 0)),
            pl.BlockSpec((block, PAIR), lambda j: (j, 0)),
        ],
        out_specs=pl.BlockSpec((block, PAIR), lambda j: (j, 0)),
        scratch_shapes=[
            pltpu.VMEM((PAIR, rows), BF16),
            pltpu.VMEM((PAIR, rows), BF16),
            pltpu.VMEM((rows, PAIR), BF16),
            pltpu.VMEM((rows, PAIR), BF16),
            pltpu.VMEM((block, rows), F32),
            pltpu.VMEM((block, rows), F32),
        ],
        compiler_params=params(),
        name="cross_attention",
    )(kv, q)


def window_kernel(block, edge, q, key_low, key_own, key_high, value_low, value_own, value_high, out, bias):
    nodes = q.shape[0]
    half = key_low.shape[0]
    wide = block + 2 * half
    first = edge[0]
    last = edge[1]

    @pl.when(pl.program_id(0) == 0)
    def _():
        row = lax.broadcasted_iota(jnp.int32, (block, wide), 0)
        column = lax.broadcasted_iota(jnp.int32, (block, wide), 1)
        near = (column >= row) & (column <= row + 2 * half)
        for b in range(nodes // block):
            there = (column + b * block >= first) & (column + b * block < last)
            bias[b] = jnp.where(near & there, 0.0, MASKED)

    keys = jnp.concatenate([key_low[...], key_own[...], key_high[...]], axis=0)
    values = jnp.concatenate([value_low[...], value_own[...], value_high[...]], axis=0).astype(F32)
    low_keys = lax.broadcasted_iota(jnp.int32, values.shape, 1) < HEAD
    v0 = jnp.where(low_keys, values, 1.0).astype(BF16)
    v1 = jnp.where(low_keys, 1.0, values).astype(BF16)
    low = lax.broadcasted_iota(jnp.int32, (block, PAIR), 1) < HEAD
    for b in range(nodes // block):
        both = q[b * block : (b + 1) * block, :].astype(F32)
        q0 = jnp.where(low, both, 0.0).astype(BF16)
        q1 = jnp.where(low, 0.0, both).astype(BF16)
        near = slice(b * block, b * block + wide)
        a0 = lax.dot_general(q0, keys[near], NT, preferred_element_type=F32) + bias[b]
        a1 = lax.dot_general(q1, keys[near], NT, preferred_element_type=F32) + bias[b]
        p0 = jnp.exp2(a0 - jnp.max(a0, axis=1, keepdims=True)).astype(BF16)
        p1 = jnp.exp2(a1 - jnp.max(a1, axis=1, keepdims=True)).astype(BF16)
        t0 = jnp.dot(p0, v0[near], preferred_element_type=F32)
        t1 = jnp.dot(p1, v1[near], preferred_element_type=F32)
        sums = pltpu.roll(jnp.where(low, t1, t0), HEAD, 1)
        out[b * block : (b + 1) * block, :] = (jnp.where(low, t0, t1) / sums).astype(BF16)


def window_attention(edge, proj, low, high, block=128):
    nodes = proj.shape[0]
    half = low.shape[0]
    pairs = GROUPS
    return pl.pallas_call(
        functools.partial(window_kernel, block),
        grid=(pairs,),
        out_shape=jax.ShapeDtypeStruct((nodes, pairs * PAIR), BF16),
        in_specs=[
            pl.BlockSpec(memory_space=pltpu.SMEM),
            pl.BlockSpec((nodes, PAIR), lambda j: (0, j)),
            pl.BlockSpec((half, PAIR), lambda j: (0, j)),
            pl.BlockSpec((nodes, PAIR), lambda j: (0, j + pairs)),
            pl.BlockSpec((half, PAIR), lambda j: (0, j)),
            pl.BlockSpec((half, PAIR), lambda j: (0, j + pairs)),
            pl.BlockSpec((nodes, PAIR), lambda j: (0, j + 2 * pairs)),
            pl.BlockSpec((half, PAIR), lambda j: (0, j + pairs)),
        ],
        out_specs=pl.BlockSpec((nodes, PAIR), lambda j: (0, j)),
        scratch_shapes=[pltpu.VMEM((nodes // block, block, block + 2 * half), F32)],
        compiler_params=params(),
        name="window_attention",
    )(edge, proj, low, proj, high, low, proj, high)


def shards(
    latent,
    observations,
    counts,
    cross_query,
    cross_kv,
    cross_out,
    self_qkv,
    self_out,
    mlp_in,
    mlp_out,
):
    nodes, width = latent.shape
    weight_in = lax.all_gather(mlp_in, LOC_STREAM, axis=1, tiled=True)
    weight_back = lax.all_gather(mlp_out, LOC_STREAM, axis=1, tiled=True)
    kv, q = project(
        counts.reshape(-1), observations.reshape(-1, width), latent, cross_kv, cross_query
    )
    kv_here, q_here = exchange(kv.reshape(LOC * GROUPS, CAP, 2 * PAIR), q)
    ctx = cross_attention(
        kv_here.reshape(-1, 2 * PAIR), q_here.reshape(-1, PAIR)
    )
    ctx = give_back(ctx.reshape(GROUPS, nodes, PAIR))
    cross_ctx = jnp.transpose(ctx, (1, 0, 2)).reshape(nodes, width)
    after_cross = (
        latent.astype(F32) + jnp.dot(cross_ctx, cross_out, preferred_element_type=F32)
    ).astype(BF16)
    proj = jnp.dot(rms_norm(after_cross), self_qkv, preferred_element_type=F32)
    scale = jnp.where(lax.broadcasted_iota(jnp.int32, (1, 3 * width), 1) < width, QSCALE, 1.0)
    proj = (proj * scale).astype(BF16)
    half = WIN // 2
    me = lax.axis_index(LOC_STREAM)
    count = LOC * GROUPS
    up = [(i, i + 1) for i in range(count - 1)]
    down = [(i + 1, i) for i in range(count - 1)]
    low = lax.ppermute(proj[nodes - half :, width:], LOC_STREAM, up)
    high = lax.ppermute(proj[:half, width:], LOC_STREAM, down)
    edge = jnp.stack(
        [jnp.where(me == 0, half, 0), jnp.where(me == count - 1, half + nodes, nodes + WIN)]
    ).astype(jnp.int32)
    self_ctx = window_attention(edge, proj, low, high)
    after_self = (
        after_cross.astype(F32) + jnp.dot(self_ctx, self_out, preferred_element_type=F32)
    ).astype(BF16)
    hidden = jax.nn.gelu(
        jnp.dot(rms_norm(after_self), weight_in, preferred_element_type=F32), approximate=True
    ).astype(BF16)
    mlp_sum = lax.dot_general(hidden, weight_back, NT, preferred_element_type=F32)
    return (after_self.astype(F32) + mlp_sum).astype(BF16)


def solution(mesh):
    finer = Mesh(mesh.devices.reshape(LOC, 4, 2), LOC_STREAM)
    return jax.shard_map(
        shards,
        mesh=finer,
        in_specs=(
            P(LOC_STREAM, None),
            P(STREAM, "loc", None, None, None),
            P(STREAM, "loc", None),
            P(),
            P(),
            P(),
            P(),
            P(),
            P(None, LOC_STREAM),
            P(None, LOC_STREAM),
        ),
        out_specs=P(LOC_STREAM, None),
        check_vma=False,
    )
```

time: 332 us -> 226 us (0.68)
  Pallas kernels: 0 us -> 155 us
  matrix products: 151 us -> 24.4 us
  waiting for transfers between devices: 60.3 us -> 15.7 us
  local copies, waits for them, and re-layouts: 41.7 us -> 6.35 us
  starting transfers between devices: 36.6 us -> 9.99 us
  blocking collectives: 19.6 us -> 0 us
  other arithmetic: 6.6 us -> 0.67 us
    pallas_call x0 -> x5, Pallas kernels: none -> 155 us  [the longest x1 66.1 us: cross_attention(): pl.pallas_call(functools.partial(cross_kernel, tile), grid=(nodes // bloc...]
    sub x7 -> x0, matrix products: 74 us -> none  [the longest x6 61 us: attend(): exp_terms = jnp.where(allowed, jnp.exp(score_matrix - block_max), 0.0)]
    dot_general x13 -> x4, matrix products: 77 us -> 24.4 us  [the longest x1 13.8 us: shards(): lax.dot_general(hidden, weight_back, NT, preferred_element_type=F32)]
    all_to_all x5 -> x0, waiting for transfers between devices: 51.1 us -> none  [the longest x1 29.2 us: shards(): lax.all_to_all(kv_split, STREAM, split_axis=2, concat_axis=0, tiled=True)]
    all_to_all x5 -> x0, starting transfers between devices: 26.2 us -> none  [the longest x1 7.39 us: shards(): lax.all_to_all(counts.astype(jnp.bfloat16), 'loc', split_axis=2, concat_a...]
    all_to_all x2 -> x0, blocking collectives: 19.6 us -> none  [exchange_in_order(): lax.all_to_all(tiles, axes[k], split_axis=k, concat_axis=k, tiled=True)]
    slice x11 -> x1, local copies, waits for them, and re-layouts: 19.4 us -> 1.61 us  [shards(): high = lax.ppermute(proj[:half, width:], LOC_STREAM, down)]
    ppermute x2, waiting for transfers between devices: 7.93 us -> 14.3 us  [the longest x1 14.3 us: shards(): low = lax.ppermute(proj[nodes - half:, width:], LOC_STREAM, up)]
  transfers between devices with their start and end apart: 9 -> 4, of which waited for: 7 -> 1; matrix products, arithmetic and copies ran while one was open for 56% -> 7% of each run, Pallas kernels for 0% -> 69%
where the time goes in v1:
time: 226 us
  Pallas kernels  155 us (69%)
  matrix products  24.4 us (11%)
  waiting for transfers between devices  15.7 us (7%)
  between operations  13.5 us (6%)
  starting transfers between devices  9.99 us (4%)
  local copies, waits for them, and re-layouts  6.35 us (3%)
    pallas_call x1, Pallas kernels, cross_attention(): pl.pallas_call(functools.partial(cross_kernel, tile), grid=(nodes // bloc...  66.1 us
    pallas_call x1, Pallas kernels, exchange(): pl.pallas_call(exchange_kernel, out_shape=(jax.ShapeDtypeStruct(kv.shape,...  47.5 us
    pallas_call x1, Pallas kernels, give_back(): pl.pallas_call(give_back_kernel, out_shape=jax.ShapeDtypeStruct(ctx.shape...  19.9 us
    ppermute x1, waiting for transfers between devices, shards(): low = lax.ppermute(proj[nodes - half:, width:], LOC_STREAM, up)  14.3 us
    dot_general x1, matrix products, shards(): lax.dot_general(hidden, weight_back, NT, preferred_element_type=F32)  13.8 us
    pallas_call x1, Pallas kernels, window_attention(): pl.pallas_call(functools.partial(window_kernel, block), grid=(pairs,), ou...  13.2 us
    pallas_call x1, Pallas kernels, project(): pl.pallas_call(project_kernel, grid=(steps,), out_shape=(jax.ShapeDtypeSt...  8.24 us
    dot_general x1, matrix products, shards(): proj = jnp.dot(rms_norm(after_cross), self_qkv, preferred_element_type=F32)  6.02 us
  transfers between devices with their start and end apart: 4, of which 1 were waited for; matrix products, arithmetic and copies ran while one was open for 7% of the time, Pallas kernels for 69%

profile of v1, /device:TPU:8, one launch (start us, length us, event | category | flops | bytes accessed | tf_op | source)
XLA Modules:
  0.0 225.6 jit_solution(15168807868193725328)
XLA Ops:
  6.5 0.7 all-gather.3.cloned.1.call-update
  7.3 0.0 all-gather.5.cloned.1.call-start
  7.3 0.7 all-gather.5.cloned.1.call-update
  8.0 8.2 %project.1 = (bf16[16,8,32,256]{3,2,1,0:T(8,128)(2,1)}, bf16[8,384,128]{2,1,0:T(8,128)(2,1)}) custom-call(s32[16]{0:T(128)} %bitcast.24, bf16[512,1024]{1,0:T(8,128)(2,1)} %bitcast.22, bf16[384,1024]{1,0:T(8,128)(2,1)} %latent.1, bf16[1024,2048]{1,0:T(8,128)(2,1)} %wv.1, bf16[1024,2048]{1,0:T(8,128)(2,1)} %wv.1, bf16[1024,1024]{1,0:T(8,128)(2,1)} %wq.1), custom_call_target="tpu_custom_call" | custom-call | tf_op jit(solution)/shard_map/project/pallas_call | solution.py:70
  16.2 47.5 %exchange.1 = (bf16[128,32,256]{2,1,0:T(8,128)(2,1)}, bf16[8,384,128]{2,1,0:T(8,128)(2,1)}) custom-call(bf16[128,32,256]{2,1,0:T(8,128)(2,1)} %bitcast.21, bf16[8,384,128]{2,1,0:T(8,128)(2,1)} %get-tuple-element.10.q), custom_call_target="tpu_custom_call" | custom-call | tf_op jit(solution)/shard_map/exchange/pallas_call | solution.py:137
  63.8 0.0 copy-start.3
  63.8 66.1 %cross_attention.1 = bf16[3072,128]{1,0:T(8,128)(2,1)} custom-call(bf16[4096,256]{1,0:T(8,128)(2,1)} %bitcast.20, bf16[3072,128]{1,0:T(8,128)(2,1)} %bitcast.23), custom_call_target="tpu_custom_call" | custom-call | tf_op jit(solution)/shard_map/cross_attention/pallas_call | solution.py:257
  129.9 19.9 %give_back.1 = bf16[8,384,128]{2,1,0:T(8,128)(2,1)} custom-call(bf16[8,384,128]{2,1,0:T(8,128)(2,1)} %bitcast.17), custom_call_target="tpu_custom_call" | custom-call | tf_op jit(solution)/shard_map/give_back/pallas_call | solution.py:173
  149.8 2.3 %copy.11 = bf16[384,8,128]{0,2,1:T(8,128)(2,1)} copy(bf16[384,8,128]{2,0,1:T(8,128)(2,1)} %bitcast.18) | data formatting | bytes 1572864 | tf_op jit(solution)/shard_map/transpose | solution.py:364
  152.1 2.3 %fusion.14 = (f32[384]{0:T(512)S(1)}, bf16[384,1024]{1,0:T(8,128)(2,1)S(1)}) fusion(bf16[384,1024]{0,1:T(8,128)(2,1)} %bitcast.19, bf16[1024,1024]{1,0:T(8,128)(2,1)S(1)} %copy-done, bf16[384,1024]{1,0:T(8,128)(2,1)S(1)} %copy-done.3), kind=kOutput, calls=%fused_computation.21 | convolution fusion | flops 807665280 | bytes 4457984 | tf_op jit(solution)/shard_map/dot_general | solution.py:366
  154.4 6.0 %multiply_convert_fusion.q.key_own.value_own = bf16[384,3072]{1,0:T(8,128)(2,1)S(1)} fusion(bf16[1024,3072]{1,0:T(8,128)(2,1)} %param.16, f32[3072]{0:T(1024)S(1)} %fusion.32, bf16[384,1024]{1,0:T(8,128)(2,1)S(1)} %get-tuple-element.16, f32[384]{0:T(512)S(1)} %add_rsqrt_fusion.1), kind=kOutput, calls=%fused_computation.9 | convolution fusion | flops 2419458048 | bytes 9451008 | tf_op jit(solution)/shard_map/dot_general | solution.py:368
  160.4 1.4 copy-done.1
  161.8 1.6 fusion.37
  163.5 4.0 %collective-permute-start = (bf16[256,2048]{1,0:T(8,128)(2,1)}, bf16[256,2048]{1,0:T(8,128)(2,1)S(1)}, u32[]{:S(2)}, u32[]{:S(2)}) collective-permute-start(bf16[256,2048]{1,0:T(8,128)(2,1)} %get-tuple-element.14), channel_id=1, source_target_pairs={{0,1},{1,2},{2,3},{3,4},{4,5},{5,6},{6,7},{7,8},{8,9},{9,10},{10,1... | collective-permute-start | bytes 3145736 | tf_op jit(solution)/shard_map/ppermute | solution.py:376
  167.5 5.9 %collective-permute-start.1 = (bf16[256,2048]{1,0:T(8,128)(2,1)}, bf16[256,2048]{1,0:T(8,128)(2,1)}, u32[]{:S(2)}, u32[]{:S(2)}) collective-permute-start(bf16[256,2048]{1,0:T(8,128)(2,1)} %get-tuple-element.13), channel_id=1, source_target_pairs={{1,0},{2,1},{3,2},{4,3},{5,4},{6,5},{7,6},{8,7},{9,8},{10,9},{11,1... | collective-permute-start | bytes 3145736 | tf_op jit(solution)/shard_map/ppermute | solution.py:377
  173.4 0.7 pad_add_fusion.edge
  174.1 14.3 %collective-permute-done.key_low.value_low = bf16[256,2048]{1,0:T(8,128)(2,1)S(1)} collective-permute-done((bf16[256,2048]{1,0:T(8,128)(2,1)}, bf16[256,2048]{1,0:T(8,128)(2,1)S(1)}, u32[]{:S(2)}, u32[]{:S(2)}) %collective-permute-start) | collective-permute-done | bytes 1048608 | tf_op jit(solution)/shard_map/ppermute | solution.py:376
  188.4 0.0 collective-permute-done.1.key_high.value_high
  188.4 1.0 copy-done.2
  189.4 13.2 %window_attention.1 = bf16[384,1024]{1,0:T(8,128)(2,1)} custom-call(s32[2]{0:T(128)} %pad_add_fusion.edge, bf16[384,3072]{1,0:T(8,128)(2,1)} %copy-done.1, bf16[256,2048]{1,0:T(8,128)(2,1)} %copy-done.2, bf16[384,3072]{1,0:T(8,128)(2,1)} %copy-done.1, bf16[256,2048]{1,0:T(8,128)(2,1)} %collective-permute-done.1.key_high.value_high, ...), custom_call_target="tpu_custom_call" | custom-call | tf_op jit(solution)/shard_map/window_attention/pallas_call | solution.py:320
  202.6 2.3 %fusion.17 = (f32[384]{0:T(512)S(1)}, bf16[384,1024]{1,0:T(8,128)(2,1)S(1)}) fusion(bf16[384,1024]{1,0:T(8,128)(2,1)} %window_attention.1, bf16[1024,1024]{1,0:T(8,128)(2,1)S(1)} %copy-done.6, bf16[384,1024]{1,0:T(8,128)(2,1)S(1)} %copy-done.5), kind=kOutput, calls=%fused_computation.24 | convolution fusion | flops 807665280 | bytes 4457984 | tf_op jit(solution)/shard_map/dot_general | solution.py:383
  204.9 0.0 all-gather.3.cloned.1.call-done
  204.9 0.0 all-gather.5.cloned.1.call-done
  204.9 13.8 %fusion.19 = bf16[384,1024]{1,0:T(8,128)(2,1)} fusion(bf16[384,1024]{1,0:T(8,128)(2,1)S(1)} %get-tuple-element.18, bf16[1024,4096]{0,1:T(8,128)(2,1)} %all-gather.5.cloned.1.call-done, bf16[1024,4096]{0,1:T(8,128)(2,1)} %all-gather.3.cloned.1.call-done, f32[384]{0:T(512)S(1)} %add_rsqrt_fusion), kind=kOutput, calls=%fused_computation.26 | convolution fusion | flops 6458966016 | bytes 18351616 | tf_op jit(solution)/shard_map/dot_general | solution.py:388
  (15 shorter events, 0.0 us)
Async XLA Ops:
  6.5 145.6 %copy-start = (bf16[1024,1024]{1,0:T(8,128)(2,1)S(1)}, bf16[1024,1024]{1,0:T(8,128)(2,1)}, u32[]{:S(2)}) copy-start(bf16[1024,1024]{1,0:T(8,128)(2,1)} %param.15) | copy-start | bytes 6291460
  6.5 198.3 %all-gather.3.cloned.1.call-start = ((), (), s32[]{:S(2)}) async-start(), calls=%async_computation | async-start | bytes 8454144 | tf_op jit(solution)/shard_map/all_gather | solution.py:354
  7.3 197.7 %all-gather.5.cloned.1.call-start = ((), (), s32[]{:S(2)}) async-start(), calls=%async_computation.1 | async-start | bytes 8454144 | tf_op jit(solution)/shard_map/all_gather | solution.py:355
  63.8 88.3 %copy-start.3 = (bf16[384,1024]{1,0:T(8,128)(2,1)S(1)}, bf16[384,1024]{1,0:T(8,128)(2,1)}, u32[]{:S(2)}) copy-start(bf16[384,1024]{1,0:T(8,128)(2,1)} %latent.1) | copy-start | bytes 2359300
  154.4 6.0 %copy-start.4 = (bf16[384,1024]{1,0:T(8,128)(2,1)}, bf16[384,1024]{1,0:T(8,128)(2,1)S(1)}, u32[]{:S(2)}) copy-start(bf16[384,1024]{1,0:T(8,128)(2,1)S(1)} %get-tuple-element.16) | copy-start | bytes 2359300
  160.4 1.4 copy-start.1
  163.5 24.9 %collective-permute-start = (bf16[256,2048]{1,0:T(8,128)(2,1)}, bf16[256,2048]{1,0:T(8,128)(2,1)S(1)}, u32[]{:S(2)}, u32[]{:S(2)}) collective-permute-start(bf16[256,2048]{1,0:T(8,128)(2,1)} %get-tuple-element.14), channel_id=1, source_target_pairs={{0,1},{1,2},{2,3},{3,4},{4,5},{5,6},{6,7},{7,8},{8,9},{9,10},{10,1... | collective-permute-start | bytes 3145736 | tf_op jit(solution)/shard_map/ppermute | solution.py:376
  167.5 20.9 %collective-permute-start.1 = (bf16[256,2048]{1,0:T(8,128)(2,1)}, bf16[256,2048]{1,0:T(8,128)(2,1)}, u32[]{:S(2)}, u32[]{:S(2)}) collective-permute-start(bf16[256,2048]{1,0:T(8,128)(2,1)} %get-tuple-element.13), channel_id=1, source_target_pairs={{1,0},{2,1},{3,2},{4,3},{5,4},{6,5},{7,6},{8,7},{9,8},{10,9},{11,1... | collective-permute-start | bytes 3145736 | tf_op jit(solution)/shard_map/ppermute | solution.py:377
  174.1 28.5 %copy-start.5 = (bf16[384,1024]{1,0:T(8,128)(2,1)S(1)}, bf16[384,1024]{1,0:T(8,128)(2,1)}, u32[]{:S(2)}) copy-start(bf16[384,1024]{1,0:T(8,128)(2,1)} %copy-done.4) | copy-start | bytes 2359300
  174.1 28.5 %copy-start.6 = (bf16[1024,1024]{1,0:T(8,128)(2,1)S(1)}, bf16[1024,1024]{1,0:T(8,128)(2,1)}, u32[]{:S(2)}) copy-start(bf16[1024,1024]{1,0:T(8,128)(2,1)} %param.17) | copy-start | bytes 6291460
  188.4 1.0 copy-start.2
Sparse Core Ops, SparseCore 0:
  10.3 94.4 all-gather.2
  107.8 70.6 all-gather.4

commit v2 on v1

--- a/solution.py
+++ b/solution.py
@@ -181,6 +181,11 @@
     )(ctx)
 
 
+PACK = 512
+SIZES = (1024, 1536, 1792, 2048, 2304, 2560, 2816, 3072, 3584, 4096)
+SPARE = 1024
+
+
 def lane_max(scores, width):
     top = scores[:, 0:PAIR]
     for c in range(1, width // PAIR):
@@ -188,21 +193,44 @@
     return top
 
 
-def cross_kernel(tile, kv, q, out, k0, k1, v0, v1, s0, s1):
-    rows = kv.shape[0]
+def pack_rows(kv, packed):
+    row = lax.broadcasted_iota(jnp.int32, (PACK, PACK), 0)
+    column = lax.broadcasted_iota(jnp.int32, (PACK, PACK), 1)
+    slot = lax.broadcasted_iota(jnp.int32, (PACK, 2 * PAIR), 0)
+    ones = jnp.ones((8, PACK), BF16)
+    end = 0
+    for g in range(kv.shape[0] // PACK):
+        rows = kv[g * PACK : (g + 1) * PACK, :]
+        live = rows[:, 0:1].astype(F32) < PADDING_FROM
+        number = jnp.sum(live.astype(F32)).astype(jnp.int32)
+        before = jnp.dot(ones, (live & (row < column)).astype(BF16), preferred_element_type=F32)
+        itself = jnp.dot(ones, (live & (row == column)).astype(BF16), preferred_element_type=F32)
+        place = jnp.where(itself > 0.5, before, -1.0)[0:1, :].astype(jnp.int32)
+        pick = (place == row).astype(BF16)
+        found = jnp.dot(pick, rows, preferred_element_type=F32)
+        packed[pl.ds(pl.multiple_of(end, 16), PACK), :] = jnp.where(
+            slot < number, found, PADDING
+        ).astype(BF16)
+        end = end + (number + 15) // 16 * 16
+    packed[pl.ds(pl.multiple_of(end, 16), SPARE), :] = jnp.full((SPARE, 2 * PAIR), PADDING, BF16)
+    return end
+
+
+def cross_kernel(kv, q, out, packed, k0, k1, v0, v1, s0, s1, length):
     block = q.shape[0]
 
     @pl.when(pl.program_id(0) == 0)
     def _():
-        prep = 512
-        lane = lax.broadcasted_iota(jnp.int32, (prep, PAIR), 1)
+        end = pack_rows(kv, packed)
+        length[0] = end
+        lane = lax.broadcasted_iota(jnp.int32, (PACK, PAIR), 1)
         low = lane < HEAD
 
-        @pl.loop(0, rows // prep)
+        @pl.loop(0, jnp.maximum((end + PACK - 1) // PACK, SIZES[0] // PACK))
         def _(b):
-            at = pl.ds(pl.multiple_of(b * prep, prep), prep)
-            key = kv[at, 0:PAIR].astype(F32)
-            value = kv[at, PAIR:].astype(F32)
+            at = pl.ds(pl.multiple_of(b * PACK, PACK), PACK)
+            key = packed[at, 0:PAIR].astype(F32)
+            value = packed[at, PAIR:].astype(F32)
             live = key < PADDING_FROM
             bias = jnp.where(live, 0.0, MASKED)
             key = jnp.where(live, key, 0.0)
@@ -214,48 +242,50 @@
             v0[at, :] = jnp.where(low, value, 1.0).astype(BF16)
             v1[at, :] = jnp.where(low, 1.0, value).astype(BF16)
 
-    lane = lax.broadcasted_iota(jnp.int32, (block, PAIR), 1)
-    low = lane < HEAD
-    both = q[...].astype(F32)
-    q0 = jnp.where(low, both, jnp.where(lane == HEAD, 1.0, 0.0)).astype(BF16)
-    q1 = jnp.where(low, jnp.where(lane == 0, 1.0, 0.0), both).astype(BF16)
-    lowest = jnp.full((block, PAIR), -3e38, F32)
-
-    def score(b, tops):
-        at = pl.ds(pl.multiple_of(b * tile, tile), tile)
-        a0 = jnp.dot(q0, k0[:, at], preferred_element_type=F32)
-        s0[:, at] = a0
-        a1 = jnp.dot(q1, k1[:, at], preferred_element_type=F32)
-        s1[:, at] = a1
-        return (
-            jnp.maximum(tops[0], lane_max(a0, tile)),
-            jnp.maximum(tops[1], lane_max(a1, tile)),
-        )
-
-    tops = lax.fori_loop(0, rows // tile, score, (lowest, lowest))
-    m0 = jnp.max(tops[0], axis=1, keepdims=True)
-    m1 = jnp.max(tops[1], axis=1, keepdims=True)
-
-    def mix(b, totals):
-        at = pl.ds(pl.multiple_of(b * tile, tile), tile)
-        p0 = jnp.exp2(s0[:, at] - m0).astype(BF16)
-        p1 = jnp.exp2(s1[:, at] - m1).astype(BF16)
-        return (
-            totals[0] + jnp.dot(p0, v0[at, :], preferred_element_type=F32),
-            totals[1] + jnp.dot(p1, v1[at, :], preferred_element_type=F32),
-        )
-
-    zero = jnp.zeros((block, PAIR), F32)
-    t0, t1 = lax.fori_loop(0, rows // tile, mix, (zero, zero))
-    sums = pltpu.roll(jnp.where(low, t1, t0), HEAD, 1)
-    out[...] = (jnp.where(low, t0, t1) / sums).astype(BF16)
-
-
-def cross_attention(kv, q, block=256, tile=512):
+    end = length[0]
+
+    def attend(size):
+        lane = lax.broadcasted_iota(jnp.int32, (block, PAIR), 1)
+        low = lane < HEAD
+        both = q[...].astype(F32)
+        q0 = jnp.where(low, both, jnp.where(lane == HEAD, 1.0, 0.0)).astype(BF16)
+        q1 = jnp.where(low, jnp.where(lane == 0, 1.0, 0.0), both).astype(BF16)
+        step = 512
+        chunks = [slice(at, min(at + step, size)) for at in range(0, size, step)]
+        lowest = jnp.full((block, PAIR), -3e38, F32)
+        zero = jnp.zeros((block, PAIR), F32)
+
+        def score(query, k, s, at, top):
+            scores = jnp.dot(query, k[:, at], preferred_element_type=F32)
+            s[:, at] = scores
+            return jnp.maximum(top, lane_max(scores, at.stop - at.start))
+
+        def mix(s, v, top, at, total):
+            weights = jnp.exp2(s[:, at] - top).astype(BF16)
+            return total + jnp.dot(weights, v[at, :], preferred_element_type=F32)
+
+        top0, top1, t0, t1 = lowest, lowest, zero, zero
+        for at in chunks:
+            top0 = score(q0, k0, s0, at, top0)
+        top0 = jnp.max(top0, axis=1, keepdims=True)
+        for at in chunks:
+            top1 = score(q1, k1, s1, at, top1)
+            t0 = mix(s0, v0, top0, at, t0)
+        top1 = jnp.max(top1, axis=1, keepdims=True)
+        for at in chunks:
+            t1 = mix(s1, v1, top1, at, t1)
+        sums = pltpu.roll(jnp.where(low, t1, t0), HEAD, 1)
+        out[...] = (jnp.where(low, t0, t1) / sums).astype(BF16)
+
+    for below, size in zip((0, *SIZES[:-1]), SIZES):
+        pl.when((end > below) & (end <= size))(functools.partial(attend, size))
+
+
+def cross_attention(kv, q, block=256):
     rows = kv.shape[0]
     nodes = q.shape[0]
     return pl.pallas_call(
-        functools.partial(cross_kernel, tile),
+        cross_kernel,
         grid=(nodes // block,),
         out_shape=jax.ShapeDtypeStruct(q.shape, BF16),
         in_specs=[
@@ -264,12 +294,14 @@
         ],
         out_specs=pl.BlockSpec((block, PAIR), lambda j: (j, 0)),
         scratch_shapes=[
+            pltpu.VMEM((rows + SPARE, 2 * PAIR), BF16),
             pltpu.VMEM((PAIR, rows), BF16),
             pltpu.VMEM((PAIR, rows), BF16),
             pltpu.VMEM((rows, PAIR), BF16),
             pltpu.VMEM((rows, PAIR), BF16),
             pltpu.VMEM((block, rows), F32),
             pltpu.VMEM((block, rows), F32),
+            pltpu.SMEM((1,), jnp.int32),
         ],
         compiler_params=params(),
         name="cross_attention",
@@ -338,6 +370,61 @@
     )(edge, proj, low, proj, high, low, proj, high)
 
 
+def tail_kernel(ctx, before, self_out, w_in, w_back, out, x, xn, total):
+    j = pl.program_id(0)
+    wide = w_in.shape[0] * w_in.shape[1]
+
+    @pl.when(j == 0)
+    def _():
+        mixed = jnp.dot(ctx[...], self_out[...], preferred_element_type=F32)
+        after = (before[...].astype(F32) + mixed).astype(BF16)
+        x[...] = after
+        xn[...] = rms_norm(after)
+
+    first = w_in[...].reshape(wide, w_in.shape[2])
+    second = w_back[...].reshape(wide, w_back.shape[2])
+    hidden = lax.dot_general(xn[...], first, NT, preferred_element_type=F32)
+    hidden = jax.nn.gelu(hidden, approximate=True).astype(BF16)
+    part = jnp.dot(hidden, second, preferred_element_type=F32)
+
+    @pl.when(j == 0)
+    def _():
+        total[...] = part
+
+    @pl.when(j > 0)
+    def _():
+        total[...] += part
+
+    @pl.when(j == pl.num_programs(0) - 1)
+    def _():
+        out[...] = (x[...].astype(F32) + total[...]).astype(BF16)
+
+
+def tail(ctx, before, self_out, weights, steps=4):
+    nodes, width = ctx.shape
+    devices, _, units, _ = weights.shape
+    return pl.pallas_call(
+        tail_kernel,
+        grid=(steps,),
+        out_shape=jax.ShapeDtypeStruct(ctx.shape, BF16),
+        in_specs=[
+            pl.BlockSpec((nodes, width), lambda j: (0, 0)),
+            pl.BlockSpec((nodes, width), lambda j: (0, 0)),
+            pl.BlockSpec((width, width), lambda j: (0, 0)),
+            pl.BlockSpec((devices // steps, None, units, width), lambda j: (j, 0, 0, 0)),
+            pl.BlockSpec((devices // steps, None, units, width), lambda j: (j, 1, 0, 0)),
+        ],
+        out_specs=pl.BlockSpec((nodes, width), lambda j: (0, 0)),
+        scratch_shapes=[
+            pltpu.VMEM((nodes, width), BF16),
+            pltpu.VMEM((nodes, width), BF16),
+            pltpu.VMEM((nodes, width), F32),
+        ],
+        compiler_params=params(),
+        name="tail",
+    )(ctx, before, self_out, weights, weights)
+
+
 def shards(
     latent,
     observations,
@@ -351,8 +438,7 @@
     mlp_out,
 ):
     nodes, width = latent.shape
-    weight_in = lax.all_gather(mlp_in, LOC_STREAM, axis=1, tiled=True)
-    weight_back = lax.all_gather(mlp_out, LOC_STREAM, axis=1, tiled=True)
+    weights = lax.all_gather(jnp.stack([mlp_in.T, mlp_out.T]), LOC_STREAM)
     kv, q = project(
         counts.reshape(-1), observations.reshape(-1, width), latent, cross_kv, cross_query
     )
@@ -379,14 +465,7 @@
         [jnp.where(me == 0, half, 0), jnp.where(me == count - 1, half + nodes, nodes + WIN)]
     ).astype(jnp.int32)
     self_ctx = window_attention(edge, proj, low, high)
-    after_self = (
-        after_cross.astype(F32) + jnp.dot(self_ctx, self_out, preferred_element_type=F32)
-    ).astype(BF16)
-    hidden = jax.nn.gelu(
-        jnp.dot(rms_norm(after_self), weight_in, preferred_element_type=F32), approximate=True
-    ).astype(BF16)
-    mlp_sum = lax.dot_general(hidden, weight_back, NT, preferred_element_type=F32)
-    return (after_self.astype(F32) + mlp_sum).astype(BF16)
+    return tail(self_ctx, after_cross, self_out, weights)
 
 
 def solution(mesh):

time: 226 us -> 185 us (0.82)
  Pallas kernels: 155 us -> 134 us
  matrix products: 24.4 us -> 8.47 us
  waiting for transfers between devices: 15.7 us -> 12 us
    pallas_call x1 -> x2, Pallas kernels: 66.1 us -> 34.4 us  [the longest x1 20.2 us: cross_attention(): pl.pallas_call(cross_kernel, grid=(nodes // block,), out_shape=jax.ShapeD...]
    dot_general x2 -> x0, matrix products: 16.1 us -> none  [the longest x1 13.8 us: shards(): lax.dot_general(hidden, weight_back, NT, preferred_element_type=F32)]
    pallas_call x1, Pallas kernels: 19.9 us -> 29.8 us  [give_back(): pl.pallas_call(give_back_kernel, out_shape=jax.ShapeDtypeStruct(ctx.shape...]
    ppermute x1, waiting for transfers between devices: 14.3 us -> 10.1 us  [shards(): low = lax.ppermute(proj[nodes - half:, width:], LOC_STREAM, up)]
  transfers between devices with their start and end apart: 4 -> 3, of which waited for: 1 -> 2; matrix products, arithmetic and copies ran while one was open for 7% -> 7% of each run, Pallas kernels for 69% -> 65%
where the time goes in v2:
time: 185 us; the launch traced here: 184 us
  Pallas kernels  134 us (72%)
  between operations  13.5 us (7%)
  waiting for transfers between devices  12 us (6%)
  starting transfers between devices  9.77 us (5%)
  matrix products  8.47 us (5%)
  local copies, waits for them, and re-layouts  4.42 us (2%)
  other arithmetic  2.32 us (1%)
    pallas_call x1, Pallas kernels, exchange(): pl.pallas_call(exchange_kernel, out_shape=(jax.ShapeDtypeStruct(kv.shape,...  48.1 us
    pallas_call x1, Pallas kernels, give_back(): pl.pallas_call(give_back_kernel, out_shape=jax.ShapeDtypeStruct(ctx.shape...  29.8 us
    pallas_call x1, Pallas kernels, cross_attention(): pl.pallas_call(cross_kernel, grid=(nodes // block,), out_shape=jax.ShapeD...  20.2 us
    pallas_call x1, Pallas kernels, tail(): pl.pallas_call(tail_kernel, grid=(steps,), out_shape=jax.ShapeDtypeStruct...  14.1 us
    pallas_call x1, Pallas kernels, window_attention(): pl.pallas_call(functools.partial(window_kernel, block), grid=(pairs,), ou...  13.2 us
    ppermute x1, waiting for transfers between devices, shards(): low = lax.ppermute(proj[nodes - half:, width:], LOC_STREAM, up)  10.1 us
    pallas_call x1, Pallas kernels, project(): pl.pallas_call(project_kernel, grid=(steps,), out_shape=(jax.ShapeDtypeSt...  8.24 us
    dot_general x1, matrix products, shards(): proj = jnp.dot(rms_norm(after_cross), self_qkv, preferred_element_type=F32)  6.22 us
  transfers between devices with their start and end apart: 3, of which 2 were waited for; matrix products, arithmetic and copies ran while one was open for 7% of the time, Pallas kernels for 65%

profile of v2, /device:TPU:8, one launch (start us, length us, event | category | flops | bytes accessed | tf_op | source)
XLA Modules:
  0.0 184.2 jit_solution(17888683141249193267)
XLA Ops:
  6.5 0.0 copy-start
  6.5 0.0 all-gather.3.cloned.1.call-start
  6.5 1.7 pad_maximum_fusion
  8.2 0.0 all-gather.3.cloned.1.call-update
  8.2 8.2 %project.1 = (bf16[16,8,32,256]{3,2,1,0:T(8,128)(2,1)}, bf16[8,384,128]{2,1,0:T(8,128)(2,1)}) custom-call(s32[16]{0:T(128)} %bitcast.31, bf16[512,1024]{1,0:T(8,128)(2,1)} %bitcast.27, bf16[384,1024]{1,0:T(8,128)(2,1)} %latent.1, bf16[1024,2048]{1,0:T(8,128)(2,1)} %wv.1, bf16[1024,2048]{1,0:T(8,128)(2,1)} %wv.1, bf16[1024,1024]{1,0:T(8,128)(2,1)} %wq.1), custom_call_target="tpu_custom_call" | custom-call | tf_op jit(solution)/shard_map/project/pallas_call | solution.py:70
  16.5 48.1 %exchange.1 = (bf16[128,32,256]{2,1,0:T(8,128)(2,1)}, bf16[8,384,128]{2,1,0:T(8,128)(2,1)}) custom-call(bf16[128,32,256]{2,1,0:T(8,128)(2,1)} %bitcast.26, bf16[8,384,128]{2,1,0:T(8,128)(2,1)} %get-tuple-element.10.q), custom_call_target="tpu_custom_call" | custom-call | tf_op jit(solution)/shard_map/exchange/pallas_call | solution.py:137
  64.6 20.2 %cross_attention.1 = bf16[3072,128]{1,0:T(8,128)(2,1)} custom-call(bf16[4096,256]{1,0:T(8,128)(2,1)} %bitcast.25, bf16[3072,128]{1,0:T(8,128)(2,1)} %bitcast.28), custom_call_target="tpu_custom_call" | custom-call | tf_op jit(solution)/shard_map/cross_attention/pallas_call | solution.py:287
  84.8 29.8 %give_back.1 = bf16[8,384,128]{2,1,0:T(8,128)(2,1)} custom-call(bf16[8,384,128]{2,1,0:T(8,128)(2,1)} %bitcast.22), custom_call_target="tpu_custom_call" | custom-call | tf_op jit(solution)/shard_map/give_back/pallas_call | solution.py:173
  114.7 2.3 %copy.12 = bf16[384,8,128]{0,2,1:T(8,128)(2,1)} copy(bf16[384,8,128]{2,0,1:T(8,128)(2,1)} %bitcast.23) | data formatting | bytes 1572864 | tf_op jit(solution)/shard_map/transpose | solution.py:450
  117.0 0.0 copy-done
  117.0 0.0 copy-done.3
  117.0 2.3 %fusion = (f32[384]{0:T(512)S(1)}, bf16[384,1024]{1,0:T(8,128)(2,1)S(1)}) fusion(bf16[384,1024]{0,1:T(8,128)(2,1)} %bitcast.24, bf16[1024,1024]{1,0:T(8,128)(2,1)S(1)} %copy-done, bf16[384,1024]{1,0:T(8,128)(2,1)S(1)} %copy-done.3), kind=kOutput, calls=%fused_computation.3 | convolution fusion | flops 807665280 | bytes 4457984 | tf_op jit(solution)/shard_map/dot_general | solution.py:452
  119.2 6.2 %multiply_convert_fusion.q.key_own.value_own = bf16[384,3072]{1,0:T(8,128)(2,1)S(1)} fusion(bf16[1024,3072]{1,0:T(8,128)(2,1)} %param.16, f32[3072]{0:T(1024)S(1)} %fusion.4, bf16[384,1024]{1,0:T(8,128)(2,1)S(1)} %get-tuple-element.16.before, f32[384]{0:T(512)S(1)} %add_rsqrt_fusion), kind=kOutput, calls=%fused_computation | convolution fusion | flops 2419458048 | bytes 9451008 | tf_op jit(solution)/shard_map/dot_general | solution.py:454
  125.5 0.0 copy-done.4
  125.5 0.0 copy-start.1
  125.5 1.8 fusion.5
  127.3 0.3 copy-done.1
  127.6 5.7 %collective-permute-start = (bf16[256,2048]{1,0:T(8,128)(2,1)}, bf16[256,2048]{1,0:T(8,128)(2,1)S(1)}, u32[]{:S(2)}, u32[]{:S(2)}) collective-permute-start(bf16[256,2048]{1,0:T(8,128)(2,1)} %get-tuple-element.14), channel_id=1, source_target_pairs={{0,1},{1,2},{2,3},{3,4},{4,5},{5,6},{6,7},{7,8},{8,9},{9,10},{10,1... | collective-permute-start | bytes 3145736 | tf_op jit(solution)/shard_map/ppermute | solution.py:462
  133.3 4.1 %collective-permute-start.1 = (bf16[256,2048]{1,0:T(8,128)(2,1)}, bf16[256,2048]{1,0:T(8,128)(2,1)}, u32[]{:S(2)}, u32[]{:S(2)}) collective-permute-start(bf16[256,2048]{1,0:T(8,128)(2,1)} %get-tuple-element.13), channel_id=1, source_target_pairs={{1,0},{2,1},{3,2},{4,3},{5,4},{6,5},{7,6},{8,7},{9,8},{10,9},{11,1... | collective-permute-start | bytes 3145736 | tf_op jit(solution)/shard_map/ppermute | solution.py:463
  137.4 0.6 pad_add_fusion.edge
  138.0 10.1 %collective-permute-done.key_low.value_low = bf16[256,2048]{1,0:T(8,128)(2,1)S(1)} collective-permute-done((bf16[256,2048]{1,0:T(8,128)(2,1)}, bf16[256,2048]{1,0:T(8,128)(2,1)S(1)}, u32[]{:S(2)}, u32[]{:S(2)}) %collective-permute-start) | collective-permute-done | bytes 1048608 | tf_op jit(solution)/shard_map/ppermute | solution.py:462
  148.1 1.9 %collective-permute-done.1.key_high.value_high = bf16[256,2048]{1,0:T(8,128)(2,1)} collective-permute-done((bf16[256,2048]{1,0:T(8,128)(2,1)}, bf16[256,2048]{1,0:T(8,128)(2,1)}, u32[]{:S(2)}, u32[]{:S(2)}) %collective-permute-start.1) | collective-permute-done | bytes 1048608 | tf_op jit(solution)/shard_map/ppermute | solution.py:463
  150.0 13.2 %window_attention.1.ctx = bf16[384,1024]{1,0:T(8,128)(2,1)} custom-call(s32[2]{0:T(128)} %pad_add_fusion.edge, bf16[384,3072]{1,0:T(8,128)(2,1)} %copy-done.1, bf16[256,2048]{1,0:T(8,128)(2,1)} %copy-done.2, bf16[384,3072]{1,0:T(8,128)(2,1)} %copy-done.1, bf16[256,2048]{1,0:T(8,128)(2,1)} %collective-permute-done.1.key_high.value_high, ...), custom_call_target="tpu_custom_call" | custom-call | tf_op jit(solution)/shard_map/window_attention/pallas_call | solution.py:352
  163.2 14.1 %tail.1 = bf16[384,1024]{1,0:T(8,128)(2,1)} custom-call(bf16[384,1024]{1,0:T(8,128)(2,1)} %window_attention.1.ctx, bf16[384,1024]{1,0:T(8,128)(2,1)} %copy-done.4, bf16[1024,1024]{1,0:T(8,128)(2,1)} %self_out.1, bf16[128,2,32,1024]{3,2,1,0:T(8,128)(2,1)} %bitcast.20, bf16[128,2,32,1024]{3,2,1,0:T(8,128)(2,1)} %bitcast.21), custom_call_target="tpu_custom_call" | custom-call | tf_op jit(solution)/shard_map/tail/pallas_call | solution.py:406
  (7 shorter events, 0.0 us)
Async XLA Ops:
  6.5 110.4 %copy-start = (bf16[1024,1024]{1,0:T(8,128)(2,1)S(1)}, bf16[1024,1024]{1,0:T(8,128)(2,1)}, u32[]{:S(2)}) copy-start(bf16[1024,1024]{1,0:T(8,128)(2,1)} %param.15) | copy-start | bytes 6291460
  6.5 156.7 %all-gather.3.cloned.1.call-start = ((), (), s32[]{:S(2)}) async-start(), calls=%async_computation | async-start | bytes 16908288 | tf_op jit(solution)/shard_map/all_gather | solution.py:441
  84.8 32.1 %copy-start.3 = (bf16[384,1024]{1,0:T(8,128)(2,1)S(1)}, bf16[384,1024]{1,0:T(8,128)(2,1)}, u32[]{:S(2)}) copy-start(bf16[384,1024]{1,0:T(8,128)(2,1)} %latent.1) | copy-start | bytes 2359300
  119.2 6.2 %copy-start.4 = (bf16[384,1024]{1,0:T(8,128)(2,1)}, bf16[384,1024]{1,0:T(8,128)(2,1)S(1)}, u32[]{:S(2)}) copy-start(bf16[384,1024]{1,0:T(8,128)(2,1)S(1)} %get-tuple-element.16.before) | copy-start | bytes 2359300
  125.5 2.1 %copy-start.1 = (bf16[384,3072]{1,0:T(8,128)(2,1)}, bf16[384,3072]{1,0:T(8,128)(2,1)S(1)}, u32[]{:S(2)}) copy-start(bf16[384,3072]{1,0:T(8,128)(2,1)S(1)} %multiply_convert_fusion.q.key_own.value_own) | copy-start | bytes 7077892
  127.6 20.5 %collective-permute-start = (bf16[256,2048]{1,0:T(8,128)(2,1)}, bf16[256,2048]{1,0:T(8,128)(2,1)S(1)}, u32[]{:S(2)}, u32[]{:S(2)}) collective-permute-start(bf16[256,2048]{1,0:T(8,128)(2,1)} %get-tuple-element.14), channel_id=1, source_target_pairs={{0,1},{1,2},{2,3},{3,4},{4,5},{5,6},{6,7},{7,8},{8,9},{9,10},{10,1... | collective-permute-start | bytes 3145736 | tf_op jit(solution)/shard_map/ppermute | solution.py:462
  133.3 16.7 %collective-permute-start.1 = (bf16[256,2048]{1,0:T(8,128)(2,1)}, bf16[256,2048]{1,0:T(8,128)(2,1)}, u32[]{:S(2)}, u32[]{:S(2)}) collective-permute-start(bf16[256,2048]{1,0:T(8,128)(2,1)} %get-tuple-element.13), channel_id=1, source_target_pairs={{1,0},{2,1},{3,2},{4,3},{5,4},{6,5},{7,6},{8,7},{9,8},{10,9},{11,1... | collective-permute-start | bytes 3145736 | tf_op jit(solution)/shard_map/ppermute | solution.py:463
  148.1 1.9 %copy-start.2 = (bf16[256,2048]{1,0:T(8,128)(2,1)}, bf16[256,2048]{1,0:T(8,128)(2,1)S(1)}, u32[]{:S(2)}) copy-start(bf16[256,2048]{1,0:T(8,128)(2,1)S(1)} %collective-permute-done.key_low.value_low) | copy-start | bytes 3145732
Sparse Core Ops, SparseCore 0:
  10.5 115.6 all-gather.2

commit v3 on v2

--- a/solution.py
+++ b/solution.py
@@ -148,37 +148,159 @@
     )(kv, q)
 
 
-def give_back_kernel(ctx, ctx_here, send, recv):
+def middle_kernel(
+    latent, ctx, cross_out, self_qkv, after, q, kv,
+    mixed, w_out, w_qkv, low, high, normed, w_sems, ctx_send, ctx_recv, send, recv,
+):
     loc = lax.axis_index("loc")
     me = lax.axis_index("s0") * 2 + lax.axis_index("s1")
-    pltpu.make_async_copy(ctx.at[me], ctx_here.at[me], recv).start()
+    flat = loc * GROUPS + me
+    nodes, width = latent.shape
+    half = low.shape[0]
+    starts, ends = flat == 0, flat == LOC * GROUPS - 1
+    outer_low = (me == 0) & jnp.logical_not(starts)
+    outer_high = (me == GROUPS - 1) & jnp.logical_not(ends)
+
+    def device(index):
+        group = lax.rem(index, GROUPS)
+        return index // GROUPS, group // 2, lax.rem(group, 2)
+
+    load_out = pltpu.make_async_copy(cross_out, w_out, w_sems.at[0])
+    load_qkv = pltpu.make_async_copy(self_qkv, w_qkv, w_sems.at[1])
+    load_out.start()
+    load_qkv.start()
+
+    barrier = pltpu.get_barrier_semaphore()
+
+    @pl.loop(1, GROUPS)
+    def _(d):
+        to = lax.rem(me + d, GROUPS)
+        pl.semaphore_signal(
+            barrier, inc=1, device_id=(loc, to // 2, lax.rem(to, 2)), device_id_type=MESH
+        )
+
+    @pl.when(outer_low)
+    def _():
+        pl.semaphore_signal(barrier, inc=1, device_id=device(flat - 1), device_id_type=MESH)
+
+    @pl.when(outer_high)
+    def _():
+        pl.semaphore_signal(barrier, inc=1, device_id=device(flat + 1), device_id_type=MESH)
+
+    pl.semaphore_wait(
+        barrier, GROUPS - 1 + outer_low.astype(jnp.int32) + outer_high.astype(jnp.int32)
+    )
+
+    place = mixed.at[:, pl.ds(pl.multiple_of(me * PAIR, PAIR), PAIR)]
 
     @pl.loop(1, GROUPS)
     def _(d):
         to = lax.rem(me + d, GROUPS)
         pltpu.make_async_remote_copy(
             ctx.at[to],
-            ctx_here.at[me],
-            send,
-            recv,
+            place,
+            ctx_send,
+            ctx_recv,
             device_id=(loc, to // 2, lax.rem(to, 2)),
             device_id_type=MESH,
         ).start()
 
-    pltpu.make_async_copy(ctx.at[pl.ds(0, GROUPS - 1)], ctx_here.at[pl.ds(0, GROUPS - 1)], send).wait()
-    pltpu.make_async_copy(ctx, ctx_here, recv).wait()
-
-
-def give_back(ctx):
+    pltpu.make_async_copy(ctx.at[me], place, ctx_recv).start()
+
+    @pl.when(starts)
+    def _():
+        low[...] = jnp.zeros_like(low)
+
+    @pl.when(ends)
+    def _():
+        high[...] = jnp.zeros_like(high)
+
+    load_out.wait()
+    pltpu.make_async_copy(mixed, mixed, ctx_recv).wait()
+    after[...] = (
+        latent[...].astype(F32) + jnp.dot(mixed[...], w_out[...], preferred_element_type=F32)
+    ).astype(BF16)
+
+    down = pltpu.make_async_remote_copy(
+        after.at[0:half], high, send.at[0], recv.at[1],
+        device_id=device(jnp.maximum(flat - 1, 0)), device_id_type=MESH,
+    )
+    up = pltpu.make_async_remote_copy(
+        after.at[nodes - half : nodes], low, send.at[1], recv.at[0],
+        device_id=device(jnp.minimum(flat + 1, LOC * GROUPS - 1)), device_id_type=MESH,
+    )
+    pl.when(jnp.logical_not(starts))(down.start)
+    pl.when(jnp.logical_not(ends))(up.start)
+
+    normed[...] = rms_norm(after[...])
+    load_qkv.wait()
+    step = 512
+
+    @pl.loop(0, width // step)
+    def _(c):
+        at = pl.ds(pl.multiple_of(c * step, step), step)
+        found = jnp.dot(normed[...], w_qkv[:, at], preferred_element_type=F32)
+        q[:, at] = (found * QSCALE).astype(BF16)
+
+    def project(rows, to):
+        @pl.loop(0, 2 * width // step)
+        def _(c):
+            at = pl.ds(pl.multiple_of(c * step, step), step)
+            weights = w_qkv[:, pl.ds(pl.multiple_of(width + c * step, step), step)]
+            kv[to, at] = jnp.dot(rows[...], weights, preferred_element_type=F32).astype(BF16)
+
+    project(normed, slice(half, half + nodes))
+
+    @pl.when(jnp.logical_not(starts))
+    def _():
+        pltpu.make_async_copy(low, low, recv.at[0]).wait()
+
+    normed[0:half] = rms_norm(low[...])
+    project(normed.at[0:half], slice(0, half))
+
+    @pl.when(jnp.logical_not(ends))
+    def _():
+        pltpu.make_async_copy(high, high, recv.at[1]).wait()
+
+    normed[0:half] = rms_norm(high[...])
+    project(normed.at[0:half], slice(half + nodes, 2 * half + nodes))
+
+    pl.when(jnp.logical_not(starts))(down.wait_send)
+    pl.when(jnp.logical_not(ends))(up.wait_send)
+    sent = ctx.at[pl.ds(0, GROUPS - 1)]
+    pltpu.make_async_copy(sent, sent, ctx_send).wait()
+
+
+def middle(latent, ctx, cross_out, self_qkv):
+    nodes, width = latent.shape
+    half = WIN // 2
+    vmem = pl.BlockSpec(memory_space=pltpu.VMEM)
+    away = pl.BlockSpec(memory_space=pl.ANY)
     return pl.pallas_call(
-        give_back_kernel,
-        out_shape=jax.ShapeDtypeStruct(ctx.shape, BF16),
-        in_specs=[pl.BlockSpec(memory_space=pl.ANY)],
-        out_specs=pl.BlockSpec(memory_space=pl.ANY),
-        scratch_shapes=[pltpu.SemaphoreType.DMA] * 2,
-        compiler_params=params(has_side_effects=True),
-        name="give_back",
-    )(ctx)
+        middle_kernel,
+        out_shape=(
+            jax.ShapeDtypeStruct((nodes, width), BF16),
+            jax.ShapeDtypeStruct((nodes, width), BF16),
+            jax.ShapeDtypeStruct((nodes + WIN, 2 * width), BF16),
+        ),
+        in_specs=[vmem, away, away, away],
+        out_specs=(vmem, vmem, vmem),
+        scratch_shapes=[
+            pltpu.VMEM((nodes, width), BF16),
+            pltpu.VMEM((width, width), BF16),
+            pltpu.VMEM((width, 3 * width), BF16),
+            pltpu.VMEM((half, width), BF16),
+            pltpu.VMEM((half, width), BF16),
+            pltpu.VMEM((nodes, width), BF16),
+            pltpu.SemaphoreType.DMA((2,)),
+            pltpu.SemaphoreType.DMA,
+            pltpu.SemaphoreType.DMA,
+            pltpu.SemaphoreType.DMA((2,)),
+            pltpu.SemaphoreType.DMA((2,)),
+        ],
+        compiler_params=params(has_side_effects=True, collective_id=1),
+        name="middle",
+    )(latent, ctx, cross_out, self_qkv)
 
 
 PACK = 512
@@ -308,15 +430,17 @@
     )(kv, q)
 
 
-def window_kernel(block, edge, q, key_low, key_own, key_high, value_low, value_own, value_high, out, bias):
+def window_kernel(block, q, key, value, out, bias):
     nodes = q.shape[0]
-    half = key_low.shape[0]
+    window = key.shape[0]
+    half = (window - nodes) // 2
     wide = block + 2 * half
-    first = edge[0]
-    last = edge[1]
+    me = (lax.axis_index("loc") * 4 + lax.axis_index("s0")) * 2 + lax.axis_index("s1")
 
     @pl.when(pl.program_id(0) == 0)
     def _():
+        first = jnp.where(me == 0, half, 0)
+        last = jnp.where(me == LOC * GROUPS - 1, half + nodes, window)
         row = lax.broadcasted_iota(jnp.int32, (block, wide), 0)
         column = lax.broadcasted_iota(jnp.int32, (block, wide), 1)
         near = (column >= row) & (column <= row + 2 * half)
@@ -324,19 +448,18 @@
             there = (column + b * block >= first) & (column + b * block < last)
             bias[b] = jnp.where(near & there, 0.0, MASKED)
 
-    keys = jnp.concatenate([key_low[...], key_own[...], key_high[...]], axis=0)
-    values = jnp.concatenate([value_low[...], value_own[...], value_high[...]], axis=0).astype(F32)
-    low_keys = lax.broadcasted_iota(jnp.int32, values.shape, 1) < HEAD
-    v0 = jnp.where(low_keys, values, 1.0).astype(BF16)
-    v1 = jnp.where(low_keys, 1.0, values).astype(BF16)
+    values = value[...].astype(F32)
+    low_values = lax.broadcasted_iota(jnp.int32, values.shape, 1) < HEAD
+    v0 = jnp.where(low_values, values, 1.0).astype(BF16)
+    v1 = jnp.where(low_values, 1.0, values).astype(BF16)
     low = lax.broadcasted_iota(jnp.int32, (block, PAIR), 1) < HEAD
     for b in range(nodes // block):
         both = q[b * block : (b + 1) * block, :].astype(F32)
         q0 = jnp.where(low, both, 0.0).astype(BF16)
         q1 = jnp.where(low, 0.0, both).astype(BF16)
         near = slice(b * block, b * block + wide)
-        a0 = lax.dot_general(q0, keys[near], NT, preferred_element_type=F32) + bias[b]
-        a1 = lax.dot_general(q1, keys[near], NT, preferred_element_type=F32) + bias[b]
+        a0 = lax.dot_general(q0, key[near, :], NT, preferred_element_type=F32) + bias[b]
+        a1 = lax.dot_general(q1, key[near, :], NT, preferred_element_type=F32) + bias[b]
         p0 = jnp.exp2(a0 - jnp.max(a0, axis=1, keepdims=True)).astype(BF16)
         p1 = jnp.exp2(a1 - jnp.max(a1, axis=1, keepdims=True)).astype(BF16)
         t0 = jnp.dot(p0, v0[near], preferred_element_type=F32)
@@ -345,29 +468,23 @@
         out[b * block : (b + 1) * block, :] = (jnp.where(low, t0, t1) / sums).astype(BF16)
 
 
-def window_attention(edge, proj, low, high, block=128):
-    nodes = proj.shape[0]
-    half = low.shape[0]
-    pairs = GROUPS
+def window_attention(q, kv, block=128):
+    nodes = q.shape[0]
+    window = kv.shape[0]
     return pl.pallas_call(
         functools.partial(window_kernel, block),
-        grid=(pairs,),
-        out_shape=jax.ShapeDtypeStruct((nodes, pairs * PAIR), BF16),
+        grid=(GROUPS,),
+        out_shape=jax.ShapeDtypeStruct(q.shape, BF16),
         in_specs=[
-            pl.BlockSpec(memory_space=pltpu.SMEM),
             pl.BlockSpec((nodes, PAIR), lambda j: (0, j)),
-            pl.BlockSpec((half, PAIR), lambda j: (0, j)),
-            pl.BlockSpec((nodes, PAIR), lambda j: (0, j + pairs)),
-            pl.BlockSpec((half, PAIR), lambda j: (0, j)),
-            pl.BlockSpec((half, PAIR), lambda j: (0, j + pairs)),
-            pl.BlockSpec((nodes, PAIR), lambda j: (0, j + 2 * pairs)),
-            pl.BlockSpec((half, PAIR), lambda j: (0, j + pairs)),
+            pl.BlockSpec((window, PAIR), lambda j: (0, j)),
+            pl.BlockSpec((window, PAIR), lambda j: (0, j + GROUPS)),
         ],
         out_specs=pl.BlockSpec((nodes, PAIR), lambda j: (0, j)),
-        scratch_shapes=[pltpu.VMEM((nodes // block, block, block + 2 * half), F32)],
+        scratch_shapes=[pltpu.VMEM((nodes // block, block, block + window - nodes), F32)],
         compiler_params=params(),
         name="window_attention",
-    )(edge, proj, low, proj, high, low, proj, high)
+    )(q, kv, kv)
 
 
 def tail_kernel(ctx, before, self_out, w_in, w_back, out, x, xn, total):
@@ -446,25 +563,10 @@
     ctx = cross_attention(
         kv_here.reshape(-1, 2 * PAIR), q_here.reshape(-1, PAIR)
     )
-    ctx = give_back(ctx.reshape(GROUPS, nodes, PAIR))
-    cross_ctx = jnp.transpose(ctx, (1, 0, 2)).reshape(nodes, width)
-    after_cross = (
-        latent.astype(F32) + jnp.dot(cross_ctx, cross_out, preferred_element_type=F32)
-    ).astype(BF16)
-    proj = jnp.dot(rms_norm(after_cross), self_qkv, preferred_element_type=F32)
-    scale = jnp.where(lax.broadcasted_iota(jnp.int32, (1, 3 * width), 1) < width, QSCALE, 1.0)
-    proj = (proj * scale).astype(BF16)
-    half = WIN // 2
-    me = lax.axis_index(LOC_STREAM)
-    count = LOC * GROUPS
-    up = [(i, i + 1) for i in range(count - 1)]
-    down = [(i + 1, i) for i in range(count - 1)]
-    low = lax.ppermute(proj[nodes - half :, width:], LOC_STREAM, up)
-    high = lax.ppermute(proj[:half, width:], LOC_STREAM, down)
-    edge = jnp.stack(
-        [jnp.where(me == 0, half, 0), jnp.where(me == count - 1, half + nodes, nodes + WIN)]
-    ).astype(jnp.int32)
-    self_ctx = window_attention(edge, proj, low, high)
+    after_cross, self_q, self_kv = middle(
+        latent, ctx.reshape(GROUPS, nodes, PAIR), cross_out, self_qkv
+    )
+    self_ctx = window_attention(self_q, self_kv)
     return tail(self_ctx, after_cross, self_out, weights)
 
 

time: 185 us -> 168 us (0.908); the launches traced: 184 us -> 165 us
  Pallas kernels: 134 us -> 150 us
  waiting for transfers between devices: 12 us -> 0.02 us
  starting transfers between devices: 9.77 us -> 0.01 us
  matrix products: 8.47 us -> 0 us
  local copies, waits for them, and re-layouts: 4.42 us -> 0 us
    pallas_call x2, Pallas kernels: 43.1 us -> 55.7 us  [the longest x1 42.7 us: middle(): pl.pallas_call(middle_kernel, out_shape=(jax.ShapeDtypeStruct((nodes, wid...]
    ppermute x2 -> x0, waiting for transfers between devices: 12 us -> none  [the longest x1 10.1 us: shards(): low = lax.ppermute(proj[nodes - half:, width:], LOC_STREAM, up)]
    ppermute x2 -> x0, starting transfers between devices: 9.77 us -> none  [the longest x1 5.69 us: shards(): low = lax.ppermute(proj[nodes - half:, width:], LOC_STREAM, up)]
    dot_general x2 -> x0, matrix products: 8.47 us -> none  [the longest x1 6.22 us: shards(): proj = jnp.dot(rms_norm(after_cross), self_qkv, preferred_element_type=F32)]
    pallas_call x1, Pallas kernels: 20.2 us -> 23.7 us  [cross_attention(): pl.pallas_call(cross_kernel, grid=(nodes // block,), out_shape=jax.ShapeD...]
    transpose x1 -> x0, local copies, waits for them, and re-layouts: 2.29 us -> none  [shards(): cross_ctx = jnp.transpose(ctx, (1, 0, 2)).reshape(nodes, width)]
  transfers between devices with their start and end apart: 3 -> 1, of which waited for: 2 -> 0; matrix products, arithmetic and copies ran while one was open for 7% -> 0% of each run, Pallas kernels for 65% -> 82%
where the time goes in v3:
time: 168 us; the launch traced here: 165 us
  Pallas kernels  150 us (89%)
  between operations  13.4 us (8%)
    pallas_call x1, Pallas kernels, exchange(): pl.pallas_call(exchange_kernel, out_shape=(jax.ShapeDtypeStruct(kv.shape,...  48.1 us
    pallas_call x1, Pallas kernels, middle(): pl.pallas_call(middle_kernel, out_shape=(jax.ShapeDtypeStruct((nodes, wid...  42.7 us
    pallas_call x1, Pallas kernels, cross_attention(): pl.pallas_call(cross_kernel, grid=(nodes // block,), out_shape=jax.ShapeD...  23.7 us
    pallas_call x1, Pallas kernels, tail(): pl.pallas_call(tail_kernel, grid=(steps,), out_shape=jax.ShapeDtypeStruct...  14.1 us
    pallas_call x1, Pallas kernels, window_attention(): pl.pallas_call(functools.partial(window_kernel, block), grid=(GROUPS,), o...  13 us
    pallas_call x1, Pallas kernels, project(): pl.pallas_call(project_kernel, grid=(steps,), out_shape=(jax.ShapeDtypeSt...  8.24 us
  transfers between devices with their start and end apart: 1, of which 0 were waited for; matrix products, arithmetic and copies ran while one was open for 0% of the time, Pallas kernels for 82%

profile of v3, /device:TPU:8, one launch (start us, length us, event | category | flops | bytes accessed | tf_op | source)
XLA Modules:
  0.0 164.8 jit_solution(5210211380272308978)
XLA Ops:
  6.5 0.0 all-gather.3.cloned.1.call-start
  6.5 1.5 pad_maximum_fusion
  8.1 0.0 all-gather.3.cloned.1.call-update
  8.1 8.2 %project.1 = (bf16[16,8,32,256]{3,2,1,0:T(8,128)(2,1)}, bf16[8,384,128]{2,1,0:T(8,128)(2,1)}) custom-call(s32[16]{0:T(128)} %bitcast.22, bf16[512,1024]{1,0:T(8,128)(2,1)} %bitcast.18, bf16[384,1024]{1,0:T(8,128)(2,1)} %latent.3, bf16[1024,2048]{1,0:T(8,128)(2,1)} %wv.1, bf16[1024,2048]{1,0:T(8,128)(2,1)} %wv.1, bf16[1024,1024]{1,0:T(8,128)(2,1)} %wq.1), custom_call_target="tpu_custom_call" | custom-call | tf_op jit(solution)/shard_map/project/pallas_call | solution.py:70
  16.3 48.1 %exchange.1 = (bf16[128,32,256]{2,1,0:T(8,128)(2,1)}, bf16[8,384,128]{2,1,0:T(8,128)(2,1)}) custom-call(bf16[128,32,256]{2,1,0:T(8,128)(2,1)} %bitcast.17, bf16[8,384,128]{2,1,0:T(8,128)(2,1)} %get-tuple-element.13.q), custom_call_target="tpu_custom_call" | custom-call | tf_op jit(solution)/shard_map/exchange/pallas_call | solution.py:137
  64.5 23.7 %cross_attention.1 = bf16[3072,128]{1,0:T(8,128)(2,1)} custom-call(bf16[4096,256]{1,0:T(8,128)(2,1)} %bitcast.16, bf16[3072,128]{1,0:T(8,128)(2,1)} %bitcast.19), custom_call_target="tpu_custom_call" | custom-call | tf_op jit(solution)/shard_map/cross_attention/pallas_call | solution.py:409
  88.2 42.7 %middle.1 = (bf16[384,1024]{1,0:T(8,128)(2,1)}, bf16[384,1024]{1,0:T(8,128)(2,1)}, bf16[896,2048]{1,0:T(8,128)(2,1)}) custom-call(bf16[384,1024]{1,0:T(8,128)(2,1)} %latent.3, bf16[8,384,128]{2,1,0:T(8,128)(2,1)} %bitcast.15, bf16[1024,1024]{1,0:T(8,128)(2,1)} %cross_out.1, bf16[1024,3072]{1,0:T(8,128)(2,1)} %self_qkv.1), custom_call_target="tpu_custom_call" | custom-call | tf_op jit(solution)/shard_map/middle/pallas_call | solution.py:279
  130.8 13.0 %window_attention.1.ctx = bf16[384,1024]{1,0:T(8,128)(2,1)} custom-call(bf16[384,1024]{1,0:T(8,128)(2,1)} %get-tuple-element.16.q, bf16[896,2048]{1,0:T(8,128)(2,1)} %get-tuple-element.17.key.value, bf16[896,2048]{1,0:T(8,128)(2,1)} %get-tuple-element.17.key.value), custom_call_target="tpu_custom_call" | custom-call | tf_op jit(solution)/shard_map/window_attention/pallas_call | solution.py:474
  143.9 0.0 all-gather.3.cloned.1.call-done
  143.9 14.1 %tail.1 = bf16[384,1024]{1,0:T(8,128)(2,1)} custom-call(bf16[384,1024]{1,0:T(8,128)(2,1)} %window_attention.1.ctx, bf16[384,1024]{1,0:T(8,128)(2,1)} %get-tuple-element.18.before, bf16[1024,1024]{1,0:T(8,128)(2,1)} %self_out.1, bf16[128,2,32,1024]{3,2,1,0:T(8,128)(2,1)} %bitcast.13, bf16[128,2,32,1024]{3,2,1,0:T(8,128)(2,1)} %bitcast.14), custom_call_target="tpu_custom_call" | custom-call | tf_op jit(solution)/shard_map/tail/pallas_call | solution.py:523
Async XLA Ops:
  6.5 137.3 %all-gather.3.cloned.1.call-start = ((), (), s32[]{:S(2)}) async-start(), calls=%async_computation | async-start | bytes 16908288 | tf_op jit(solution)/shard_map/all_gather | solution.py:558
Sparse Core Ops, SparseCore 0:
  10.5 119.9 all-gather.2

commit v4 on v3

--- a/solution.py
+++ b/solution.py
@@ -41,11 +41,35 @@
     )
 
 
-def project_kernel(counts, obs, latent, wk, wv, wq, kv_out, q_out, xn, ln):
-    @pl.when(pl.program_id(0) == 0)
-    def _():
+def project_kernel(
+    counts, obs, latent, wk, wv, wq, w_in, w_back, kv_out, q_out, column,
+    xn, ln, send, recv,
+):
+    loc = lax.axis_index("loc")
+    z = lax.axis_index("s0")
+    core = lax.axis_index("s1")
+    step = pl.program_id(0)
+
+    @pl.when(step == 0)
+    def _():
+        barrier = pltpu.get_barrier_semaphore()
+        for d in range(1, 4):
+            pl.semaphore_signal(
+                barrier, inc=1, device_id=(loc, lax.rem(z + d, 4), core), device_id_type=MESH
+            )
         xn[...] = rms_norm(obs[...])
         ln[...] = rms_norm(latent[...])
+
+    @pl.when(step == 1)
+    def _():
+        pl.semaphore_wait(pltpu.get_barrier_semaphore(), 3)
+        for at, part in enumerate((w_in, w_back)):
+            pltpu.make_async_copy(part, column.at[z, at], recv).start()
+            for d in range(1, 4):
+                pltpu.make_async_remote_copy(
+                    part, column.at[z, at], send, recv,
+                    device_id=(loc, lax.rem(z + d, 4), core), device_id_type=MESH,
+                ).start()
 
     q = (jnp.dot(ln[...], wq[...], preferred_element_type=F32) * QSCALE).astype(BF16)
     k = jnp.dot(xn[...], wk[...], preferred_element_type=F32)
@@ -61,8 +85,14 @@
     for g in range(2):
         q_out[g] = q[:, g * PAIR : (g + 1) * PAIR]
 
-
-def project(counts, obs, latent, cross_kv, cross_query):
+    @pl.when(step == pl.num_programs(0) - 1)
+    def _():
+        sent = column.at[pl.ds(0, 3)]
+        pltpu.make_async_copy(sent, sent, send).wait()
+        pltpu.make_async_copy(column, column, recv).wait()
+
+
+def project(counts, obs, latent, cross_kv, cross_query, w_in, w_back):
     rows, width = obs.shape
     nodes = latent.shape[0]
     step = 2 * PAIR
@@ -73,6 +103,7 @@
         out_shape=(
             jax.ShapeDtypeStruct((LOC, GROUPS, CAP, 2 * PAIR), BF16),
             jax.ShapeDtypeStruct((GROUPS, nodes, PAIR), BF16),
+            jax.ShapeDtypeStruct((4, 2, *w_in.shape), BF16),
         ),
         in_specs=[
             pl.BlockSpec(memory_space=pltpu.SMEM),
@@ -81,15 +112,23 @@
             pl.BlockSpec((width, step), lambda j: (0, j)),
             pl.BlockSpec((width, step), lambda j: (0, j + steps)),
             pl.BlockSpec((width, step), lambda j: (0, j)),
+            pl.BlockSpec(memory_space=pl.ANY),
+            pl.BlockSpec(memory_space=pl.ANY),
         ],
         out_specs=(
             pl.BlockSpec((LOC, 2, CAP, 2 * PAIR), lambda j: (0, j, 0, 0)),
             pl.BlockSpec((2, nodes, PAIR), lambda j: (j, 0, 0)),
+            pl.BlockSpec(memory_space=pl.ANY),
         ),
-        scratch_shapes=[pltpu.VMEM((rows, width), BF16), pltpu.VMEM((nodes, width), BF16)],
-        compiler_params=params(),
+        scratch_shapes=[
+            pltpu.VMEM((rows, width), BF16),
+            pltpu.VMEM((nodes, width), BF16),
+            pltpu.SemaphoreType.DMA,
+            pltpu.SemaphoreType.DMA,
+        ],
+        compiler_params=params(has_side_effects=True, collective_id=2),
         name="project",
-    )(counts, obs, latent, cross_kv, cross_kv, cross_query)
+    )(counts, obs, latent, cross_kv, cross_kv, cross_query, w_in, w_back)
 
 
 def exchange_kernel(kv, q, kv_here, q_here, kv_send, kv_recv, q_send, q_recv):
@@ -468,7 +507,7 @@
         out[b * block : (b + 1) * block, :] = (jnp.where(low, t0, t1) / sums).astype(BF16)
 
 
-def window_attention(q, kv, block=128):
+def window_attention(q, kv, block=192):
     nodes = q.shape[0]
     window = kv.shape[0]
     return pl.pallas_call(
@@ -487,59 +526,99 @@
     )(q, kv, kv)
 
 
-def tail_kernel(ctx, before, self_out, w_in, w_back, out, x, xn, total):
-    j = pl.program_id(0)
-    wide = w_in.shape[0] * w_in.shape[1]
-
-    @pl.when(j == 0)
-    def _():
-        mixed = jnp.dot(ctx[...], self_out[...], preferred_element_type=F32)
-        after = (before[...].astype(F32) + mixed).astype(BF16)
-        x[...] = after
-        xn[...] = rms_norm(after)
-
-    first = w_in[...].reshape(wide, w_in.shape[2])
-    second = w_back[...].reshape(wide, w_back.shape[2])
-    hidden = lax.dot_general(xn[...], first, NT, preferred_element_type=F32)
-    hidden = jax.nn.gelu(hidden, approximate=True).astype(BF16)
-    part = jnp.dot(hidden, second, preferred_element_type=F32)
-
-    @pl.when(j == 0)
-    def _():
-        total[...] = part
-
-    @pl.when(j > 0)
-    def _():
-        total[...] += part
-
-    @pl.when(j == pl.num_programs(0) - 1)
-    def _():
-        out[...] = (x[...].astype(F32) + total[...]).astype(BF16)
-
-
-def tail(ctx, before, self_out, weights, steps=4):
+def tail_kernel(
+    ctx, before, self_out, weights, out,
+    w_in, w_back, x, mine, other, total, part, got, w_sems, send, recv,
+):
+    loc = lax.axis_index("loc")
+    z = lax.axis_index("s0")
+    core = lax.axis_index("s1")
+    chunks, devices = w_in.shape[0], w_in.shape[1]
+    sibling = functools.partial(
+        pltpu.make_async_remote_copy, device_id=(loc, z, 1 - core), device_id_type=MESH
+    )
+
+    def load(c):
+        at = pl.ds(c * devices, devices)
+        return (
+            pltpu.make_async_copy(weights.at[at, 0], w_in.at[c], w_sems.at[0, c]),
+            pltpu.make_async_copy(weights.at[at, 1], w_back.at[c], w_sems.at[1, c]),
+        )
+
+    for c in range(chunks):
+        for copy in load(c):
+            copy.start()
+    barrier = pltpu.get_barrier_semaphore()
+    pl.semaphore_signal(barrier, inc=1, device_id=(loc, z, 1 - core), device_id_type=MESH)
+
+    mixed = jnp.dot(ctx[...], self_out[...], preferred_element_type=F32)
+    after = (before[...].astype(F32) + mixed).astype(BF16)
+    x[...] = after
+    mine[...] = rms_norm(after)
+    pl.semaphore_wait(barrier, 1)
+    give = sibling(mine, other, send.at[0], recv.at[0])
+    give.start()
+
+    def mlp(rows, c):
+        wide = devices * w_in.shape[2]
+        first = w_in[c].reshape(wide, w_in.shape[3])
+        second = w_back[c].reshape(wide, w_back.shape[3])
+        hidden = lax.dot_general(rows[...], first, NT, preferred_element_type=F32)
+        hidden = jax.nn.gelu(hidden, approximate=True).astype(BF16)
+        return jnp.dot(hidden, second, preferred_element_type=F32)
+
+    for copy in load(0):
+        copy.wait()
+    total[...] = mlp(mine, 0)
+    give.wait_recv()
+    part[...] = mlp(other, 0)
+    for c in range(1, chunks):
+        for copy in load(c):
+            copy.wait()
+
+    @pl.loop(1, chunks)
+    def _(c):
+        part[...] += mlp(other, c)
+
+    back = sibling(part, got, send.at[1], recv.at[1])
+    back.start()
+
+    @pl.loop(1, chunks)
+    def _(c):
+        total[...] += mlp(mine, c)
+
+    back.wait_recv()
+    out[...] = (x[...].astype(F32) + (total[...] + got[...])).astype(BF16)
+    give.wait_send()
+    back.wait_send()
+
+
+def tail(ctx, before, self_out, weights, chunks=4):
     nodes, width = ctx.shape
     devices, _, units, _ = weights.shape
+    vmem = pl.BlockSpec(memory_space=pltpu.VMEM)
+    block = (chunks, devices // chunks, units, width)
     return pl.pallas_call(
         tail_kernel,
-        grid=(steps,),
         out_shape=jax.ShapeDtypeStruct(ctx.shape, BF16),
-        in_specs=[
-            pl.BlockSpec((nodes, width), lambda j: (0, 0)),
-            pl.BlockSpec((nodes, width), lambda j: (0, 0)),
-            pl.BlockSpec((width, width), lambda j: (0, 0)),
-            pl.BlockSpec((devices // steps, None, units, width), lambda j: (j, 0, 0, 0)),
-            pl.BlockSpec((devices // steps, None, units, width), lambda j: (j, 1, 0, 0)),
-        ],
-        out_specs=pl.BlockSpec((nodes, width), lambda j: (0, 0)),
+        in_specs=[vmem, vmem, vmem, pl.BlockSpec(memory_space=pl.ANY)],
+        out_specs=vmem,
         scratch_shapes=[
+            pltpu.VMEM(block, BF16),
+            pltpu.VMEM(block, BF16),
+            pltpu.VMEM((nodes, width), BF16),
             pltpu.VMEM((nodes, width), BF16),
             pltpu.VMEM((nodes, width), BF16),
             pltpu.VMEM((nodes, width), F32),
+            pltpu.VMEM((nodes, width), F32),
+            pltpu.VMEM((nodes, width), F32),
+            pltpu.SemaphoreType.DMA((2, chunks)),
+            pltpu.SemaphoreType.DMA((2,)),
+            pltpu.SemaphoreType.DMA((2,)),
         ],
-        compiler_params=params(),
+        compiler_params=params(has_side_effects=True, collective_id=3),
         name="tail",
-    )(ctx, before, self_out, weights, weights)
+    )(ctx, before, self_out, weights)
 
 
 def shards(
@@ -555,10 +634,11 @@
     mlp_out,
 ):
     nodes, width = latent.shape
-    weights = lax.all_gather(jnp.stack([mlp_in.T, mlp_out.T]), LOC_STREAM)
-    kv, q = project(
-        counts.reshape(-1), observations.reshape(-1, width), latent, cross_kv, cross_query
-    )
+    kv, q, column = project(
+        counts.reshape(-1), observations.reshape(-1, width), latent, cross_kv, cross_query,
+        mlp_in.T, mlp_out.T,
+    )
+    weights = lax.all_gather(column, "loc").reshape(-1, *column.shape[1:])
     kv_here, q_here = exchange(kv.reshape(LOC * GROUPS, CAP, 2 * PAIR), q)
     ctx = cross_attention(
         kv_here.reshape(-1, 2 * PAIR), q_here.reshape(-1, PAIR)

time: 168 us -> 166 us (0.988); the launches traced: 165 us -> 165 us
  local copies, waits for them, and re-layouts: 0 us -> 2.06 us
    pallas_call x1, Pallas kernels: 8.24 us -> 15.3 us  [project(): pl.pallas_call(project_kernel, grid=(steps,), out_shape=(jax.ShapeDtypeSt...]
    pallas_call x1, Pallas kernels: 23.7 us -> 20.2 us  [cross_attention(): pl.pallas_call(cross_kernel, grid=(nodes // block,), out_shape=jax.ShapeD...]
    unnamed x0 -> x1, local copies, waits for them, and re-layouts: none -> 2.06 us
    pallas_call x1, Pallas kernels: 48.1 us -> 46.3 us  [exchange(): pl.pallas_call(exchange_kernel, out_shape=(jax.ShapeDtypeStruct(kv.shape,...]
  transfers between devices with their start and end apart: 1 -> 1, of which waited for: 0 -> 0; matrix products, arithmetic and copies ran while one was open for 0% -> 0% of each run, Pallas kernels for 82% -> 73%
where the time goes in v4:
time: 166 us; the launch traced here: 165 us
  Pallas kernels  149 us (90%)
  between operations  13.4 us (8%)
  local copies, waits for them, and re-layouts  2.06 us (1%)
    pallas_call x1, Pallas kernels, exchange(): pl.pallas_call(exchange_kernel, out_shape=(jax.ShapeDtypeStruct(kv.shape,...  46.3 us
    pallas_call x1, Pallas kernels, middle(): pl.pallas_call(middle_kernel, out_shape=(jax.ShapeDtypeStruct((nodes, wid...  41.3 us
    pallas_call x1, Pallas kernels, cross_attention(): pl.pallas_call(cross_kernel, grid=(nodes // block,), out_shape=jax.ShapeD...  20.2 us
    pallas_call x1, Pallas kernels, project(): pl.pallas_call(project_kernel, grid=(steps,), out_shape=(jax.ShapeDtypeSt...  15.3 us
    pallas_call x1, Pallas kernels, tail(): pl.pallas_call(tail_kernel, out_shape=jax.ShapeDtypeStruct(ctx.shape, BF1...  14.5 us
    pallas_call x1, Pallas kernels, window_attention(): pl.pallas_call(functools.partial(window_kernel, block), grid=(GROUPS,), o...  11.8 us
  transfers between devices with their start and end apart: 1, of which 0 were waited for; matrix products, arithmetic and copies ran while one was open for 0% of the time, Pallas kernels for 73%

profile of v4, /device:TPU:8, one launch (start us, length us, event | category | flops | bytes accessed | tf_op | source)
XLA Modules:
  0.0 165.0 jit_solution(1762434261764033752)
XLA Ops:
  6.5 0.0 all-gather.3.cloned.1.call-start
  6.5 15.3 %project.1 = (bf16[16,8,32,256]{3,2,1,0:T(8,128)(2,1)}, bf16[8,384,128]{2,1,0:T(8,128)(2,1)}, bf16[4,2,32,1024]{3,2,1,0:T(8,128)(2,1)}) custom-call(s32[16]{0:T(128)} %bitcast.15, bf16[512,1024]{1,0:T(8,128)(2,1)} %bitcast.11, bf16[384,1024]{1,0:T(8,128)(2,1)} %latent.3, bf16[1024,2048]{1,0:T(8,128)(2,1)} %wv.1, bf16[1024,2048]{1,0:T(8,128)(2,1)} %wv.1, ...), custom_call_target="tpu_custom_call" | custom-call | tf_op jit(solution)/shard_map/project/pallas_call | solution.py:100
  21.9 0.0 all-gather.3.cloned.1.call-update
  21.9 46.3 %exchange.1 = (bf16[128,32,256]{2,1,0:T(8,128)(2,1)}, bf16[8,384,128]{2,1,0:T(8,128)(2,1)}) custom-call(bf16[128,32,256]{2,1,0:T(8,128)(2,1)} %bitcast.10, bf16[8,384,128]{2,1,0:T(8,128)(2,1)} %get-tuple-element.14.q), custom_call_target="tpu_custom_call" | custom-call | tf_op jit(solution)/shard_map/exchange/pallas_call | solution.py:176
  68.2 20.2 %cross_attention.1 = bf16[3072,128]{1,0:T(8,128)(2,1)} custom-call(bf16[4096,256]{1,0:T(8,128)(2,1)} %bitcast.9, bf16[3072,128]{1,0:T(8,128)(2,1)} %bitcast.12), custom_call_target="tpu_custom_call" | custom-call | tf_op jit(solution)/shard_map/cross_attention/pallas_call | solution.py:448
  88.5 41.3 %middle.1 = (bf16[384,1024]{1,0:T(8,128)(2,1)}, bf16[384,1024]{1,0:T(8,128)(2,1)}, bf16[896,2048]{1,0:T(8,128)(2,1)}) custom-call(bf16[384,1024]{1,0:T(8,128)(2,1)} %latent.3, bf16[8,384,128]{2,1,0:T(8,128)(2,1)} %bitcast.8, bf16[1024,1024]{1,0:T(8,128)(2,1)} %cross_out.1, bf16[1024,3072]{1,0:T(8,128)(2,1)} %self_qkv.1), custom_call_target="tpu_custom_call" | custom-call | tf_op jit(solution)/shard_map/middle/pallas_call | solution.py:318
  129.8 11.8 %window_attention.1.ctx = bf16[384,1024]{1,0:T(8,128)(2,1)} custom-call(bf16[384,1024]{1,0:T(8,128)(2,1)} %get-tuple-element.17.q, bf16[896,2048]{1,0:T(8,128)(2,1)} %get-tuple-element.18.key.value, bf16[896,2048]{1,0:T(8,128)(2,1)} %get-tuple-element.18.key.value), custom_call_target="tpu_custom_call" | custom-call | tf_op jit(solution)/shard_map/window_attention/pallas_call | solution.py:513
  141.6 0.0 all-gather.3.cloned.1.call-done.weights
  141.6 14.5 %tail.1 = bf16[384,1024]{1,0:T(8,128)(2,1)} custom-call(bf16[384,1024]{1,0:T(8,128)(2,1)} %window_attention.1.ctx, bf16[384,1024]{1,0:T(8,128)(2,1)} %get-tuple-element.19.before, bf16[1024,1024]{1,0:T(8,128)(2,1)} %self_out.1, bf16[64,2,32,1024]{3,2,1,0:T(8,128)(2,1)} %all-gather.3.cloned.1.call-done.weights), custom_call_target="tpu_custom_call" | custom-call | tf_op jit(solution)/shard_map/tail/pallas_call | solution.py:601
  156.1 2.1 %copy.12 = bf16[384,1024]{1,0:T(8,128)(2,1)} copy(bf16[384,1024]{1,0:T(8,128)(2,1)} %tail.1) | data formatting | bytes 1572864
Async XLA Ops:
  6.5 135.1 %all-gather.3.cloned.1.call-start = ((), (), s32[]{:S(2)}) async-start(), calls=%async_computation | async-start | bytes 8912896 | tf_op jit(solution)/shard_map/all_gather | solution.py:641
Sparse Core Ops, SparseCore 0:
  22.0 96.4 all-gather.2
